TPU v7x, 128 devices: a whole 4x4x4 slice. The times are simulated.
128 devices in a mesh: tm: 32 (over y, z, x_hi), head: 4 (over x_lo, core).
Axes of the slice: x: 4 (x_hi: 2, x_lo: 2; x = x_hi * 2 + x_lo), y: 4, z: 4, core: 2. Of those that a mesh axis runs over, the one named last changes fastest.
Arguments:
- query: bfloat16 [4096, 2560], P('tm', 'head'), may hold values from -8 to 8
- key: bfloat16 [4096, 2560], P('tm', 'head'), may hold values from -8 to 8
- value: bfloat16 [4096, 2560], P('tm', 'head'), may hold values from -6 to 6
- grad_out: bfloat16 [4096, 2560], P('tm', 'head'), may hold values from -6 to 6
- frame_ids: int32 [32], replicated, may hold values from 0 to 8, as said below
- sink_frame: int32 [1], replicated, may hold values from 0 to 8
- window: int32 [20], P('head'), may hold values from 1 to 3, as said below
Outputs:
- attended: bfloat16 [4096, 2560], P('tm', 'head')
- query_grad: bfloat16 [4096, 2560], P('tm', 'head')
- key_grad: bfloat16 [4096, 2560], P('tm', 'head')
- value_grad: bfloat16 [4096, 2560], P('tm', 'head')
Inputs may be any that keep to these rules, and one draw needn't show every extreme that they name: frame_ids[b] = (b + c) // 4 for one c of 1 to 3: every frame is four blocks except the first and the last, which have 4 - c and c blocks. Some head has a window of 3 and some a window of 1.
All inputs are finite; a program needn't handle non-finite values.
Results may differ from a plain program's by a relative error of at most 0.033.
Values may be sent and summed in bfloat16 or wider, within the bound.
A program may use at most 128 MiB of HBM per device.

v0:
```python
import math

import jax
import jax.numpy as jnp
from jax import lax
from jax.sharding import PartitionSpec as P

masked_score = -1e30


def passed_along(value, axis, by):
    devices = lax.axis_size(axis)
    pairs = [(i, i + by) for i in range(devices) if 0 <= i + by < devices]
    return lax.ppermute(value, axis, pairs)


def broadcast(block, axis, source):
    block = jnp.where(lax.axis_index(axis) == source, block, jnp.zeros_like(block))
    return lax.psum(block, axis)


def attend(query_heads, grad_heads, key_value_parts, flag_list, scaling):
    block_rows, head_count, head_dim = query_heads.shape
    groups = []
    for first_slot in range(0, len(key_value_parts), 2):
        members = key_value_parts[first_slot : first_slot + 2]
        flag_pair = flag_list[first_slot : first_slot + 2]
        key_rows = jnp.concatenate([member[0] for member in members], axis=0).reshape(
            -1, head_count, head_dim
        )
        value_rows = jnp.concatenate([member[1] for member in members], axis=0).reshape(
            -1, head_count, head_dim
        )
        visible = jnp.concatenate(
            [jnp.broadcast_to(marker[:, None], (head_count, block_rows)) for marker in flag_pair],
            axis=1,
        )[:, None, :]
        groups.append((key_rows, value_rows, visible))
    running_max = jnp.full((head_count, block_rows), masked_score, jnp.float32)
    running_sum = jnp.zeros((head_count, block_rows), jnp.float32)
    weighted = jnp.zeros((head_count, block_rows, head_dim), jnp.float32)
    for key_rows, value_rows, visible in groups:
        scores = (
            jnp.einsum("qhd,khd->hqk", query_heads, key_rows, preferred_element_type=jnp.float32)
            * scaling
        )
        scores = jnp.where(visible, scores, masked_score)
        new_max = jnp.maximum(running_max, jnp.max(scores, axis=-1))
        factor = jnp.exp(running_max - new_max)
        weights = jnp.where(visible, jnp.exp(scores - new_max[:, :, None]), 0.0)
        running_sum = running_sum * factor + jnp.sum(weights, axis=-1)
        weighted = weighted * factor[:, :, None] + jnp.einsum(
            "hqk,khd->hqd",
            weights.astype(jnp.bfloat16),
            value_rows,
            preferred_element_type=jnp.float32,
        )
        running_max = new_max
    mixed = weighted / running_sum[:, :, None]
    attended = mixed.transpose(1, 0, 2).astype(jnp.bfloat16)
    log_total = running_max + jnp.log(running_sum)
    row_dots = jnp.sum(grad_heads.astype(jnp.float32) * attended.astype(jnp.float32), axis=-1).T
    query_grad = jnp.zeros((block_rows, head_count, head_dim), jnp.float32)
    partials = []
    for key_rows, value_rows, visible in groups:
        scores = (
            jnp.einsum("qhd,khd->hqk", query_heads, key_rows, preferred_element_type=jnp.float32)
            * scaling
        )
        weights_back = jnp.where(visible, jnp.exp(scores - log_total[:, :, None]), 0.0)
        dot_back = jnp.einsum(
            "qhd,khd->hqk", grad_heads, value_rows, preferred_element_type=jnp.float32
        )
        score_grad = (weights_back * (dot_back - row_dots[:, :, None])).astype(jnp.bfloat16)
        query_grad = query_grad + jnp.einsum(
            "hqk,khd->qhd", score_grad, key_rows, preferred_element_type=jnp.float32
        )
        key_part = (
            jnp.einsum("hqk,qhd->khd", score_grad, query_heads, preferred_element_type=jnp.float32)
            * scaling
        )
        value_part = jnp.einsum(
            "hqk,qhd->khd",
            weights_back.astype(jnp.bfloat16),
            grad_heads,
            preferred_element_type=jnp.float32,
        )
        grad_pair = jnp.stack(
            [
                key_part.reshape(-1, head_count * head_dim),
                value_part.reshape(-1, head_count * head_dim),
            ]
        )
        for k in range(grad_pair.shape[1] // block_rows):
            partials.append(grad_pair[:, k * block_rows : (k + 1) * block_rows])
    query_grad = (
        (query_grad * scaling).reshape(block_rows, head_count * head_dim).astype(jnp.bfloat16)
    )
    return (attended.reshape(block_rows, head_count * head_dim), query_grad, partials)


def per_device(query, key, value, grad_out, frame_ids, sink_frame, window):
    block_rows, row_width = query.shape
    head_count = window.shape[0]
    head_dim = row_width // head_count
    scaling = 1.0 / math.sqrt(head_dim)
    blocks = lax.axis_size("tm")
    my_block = lax.axis_index("tm")
    query_heads = query.reshape(block_rows, head_count, head_dim)
    grad_heads = grad_out.reshape(block_rows, head_count, head_dim)
    key_value = jnp.stack([key, value])
    query_frame = frame_ids[my_block]
    sink_index = sink_frame[0]
    sink_start = jnp.sum((frame_ids < sink_index).astype(jnp.int32))
    offsets = [0] + [k for k in range(1, 12)] + [-1, -2, -3]

    def near_flag(offset):
        key_block = my_block - offset
        in_range = (key_block >= 0) & (key_block < blocks)
        key_frame = frame_ids[jnp.clip(key_block, 0, blocks - 1)]
        return in_range & (key_frame <= query_frame) & (key_frame > query_frame - window)

    sink_roots = [sink_start + k for k in range(4)]
    sink_flags = [
        (root_block < blocks)
        & (frame_ids[jnp.clip(root_block, 0, blocks - 1)] == sink_index)
        & (sink_index <= query_frame - window)
        for root_block in sink_roots
    ]
    nearby = [key_value] + [passed_along(key_value, "tm", offset) for offset in offsets[1:]]
    holds_sink = query_frame == sink_index
    sink_slot = jnp.clip(my_block - sink_start, 0, 3)
    sink_parts = [
        broadcast(key_value, "tm", jnp.clip(root_block, 0, blocks - 1)) for root_block in sink_roots
    ]
    flag_list = [near_flag(offset) for offset in offsets] + sink_flags
    attended, query_grad, partials = attend(
        query_heads, grad_heads, nearby + sink_parts, flag_list, scaling
    )
    key_value_grad = partials[0]
    for offset, part in zip(offsets[1:], partials[1:15]):
        key_value_grad = key_value_grad + passed_along(
            part.astype(jnp.bfloat16), "tm", -offset
        ).astype(part.dtype)
    sink_sums = lax.psum(jnp.stack(partials[15:19]).astype(jnp.bfloat16), "tm").astype(jnp.float32)
    key_value_grad = key_value_grad + jnp.where(
        holds_sink, lax.dynamic_index_in_dim(sink_sums, sink_slot, 0, False), 0.0
    )
    key_grad = key_value_grad[0].astype(jnp.bfloat16)
    value_grad = key_value_grad[1].astype(jnp.bfloat16)
    return (attended, query_grad, key_grad, value_grad)


def solution(mesh):
    return jax.shard_map(
        per_device,
        mesh=mesh,
        in_specs=(
            P("tm", "head"),
            P("tm", "head"),
            P("tm", "head"),
            P("tm", "head"),
            P(),
            P(),
            P("head"),
        ),
        out_specs=(P("tm", "head"), P("tm", "head"), P("tm", "head"), P("tm", "head")),
        check_vma=False,
    )
```

profile of v0, /device:TPU:102, one launch (start us, length us, event | category | flops | bytes accessed | tf_op | source)
XLA Modules:
  0.0 841.7 jit_solution(5958754766825011687)
XLA Ops:
  7.9 1.3 fusion.245
  14.0 1.3 broadcast_select_fusion
  15.2 3.3 collective-permute-start.13
  18.5 2.0 collective-permute-start.12
  20.5 4.1 collective-permute-start.11
  24.6 9.3 %collective-permute-start.10 = (bf16[2,128,640]{1,2,0:T(8,128)(2,1)}, bf16[2,128,640]{1,2,0:T(8,128)(2,1)S(1)}, u32[]{:S(2)}, u32[]{:S(2)}) collective-permute-start(bf16[2,128,640]{1,2,0:T(8,128)(2,1)} %get-tuple-element.96), channel_id=1, source_target_pairs={{0,44},{4,48},{8,52},{12,56},{16,60},{20,64},{24,68},{28,72},{32,7... | collective-permute-start | bytes 983048 | tf_op jit(solution)/shard_map/ppermute | solution.py:14
  33.9 5.1 collective-permute-start.9
  65.6 3.8 compare_and_fusion.9
  69.5 5.5 compare_and_fusion.10
  76.3 1.8 collective-permute-start.8
  78.8 1.3 collective-permute-start.7
  80.8 1.9 collective-permute-start.6
  83.4 1.9 collective-permute-start.5
  86.0 2.5 collective-permute-start.4
  89.2 2.9 collective-permute-start.3
  92.8 13.3 %collective-permute-done.7 = bf16[2,128,640]{1,2,0:T(8,128)(2,1)S(1)} collective-permute-done((bf16[2,128,640]{1,2,0:T(8,128)(2,1)}, bf16[2,128,640]{1,2,0:T(8,128)(2,1)S(1)}, u32[]{:S(2)}, u32[]{:S(2)}) %collective-permute-start.7) | collective-permute-done | bytes 327712 | tf_op jit(solution)/shard_map/ppermute | solution.py:14
  106.0 4.5 collective-permute-start.2
  111.2 5.8 collective-permute-start.1
  118.4 2.1 collective-permute-start
  121.8 5.8 collective-permute-done.3
  129.0 1.7 fusion.338
  131.4 2.9 collective-permute-done.1
  134.4 1.7 fusion.337
  136.5 1.2 bitcast_reduce_fusion.4
  137.6 3.8 collective-permute-done
  141.4 1.7 fusion.339
  144.9 1.1 copy.124
  147.4 1.1 bitcast_reduce_fusion.6
  149.9 236.6 %all-reduce.6.cloned.1.call-done = (bf16[2,128,640]{1,2,0:T(8,128)(2,1)}, bf16[2,128,640]{1,2,0:T(8,128)(2,1)}, bf16[2,128,640]{1,2,0:T(8,128)(2,1)}, bf16[2,128,640]{1,2,0:T(8,128)(2,1)}) async-done(((bf16[2,128,640]{1,2,0:T(8,128)(2,1)}, bf16[2,128,640]{1,2,0:T(8,128)(2,1)}, bf16[2,128,640]{1,2,0:T(8,128)(2,1)}, bf16[2,128,640]{1,2,0:T(8,128)(2,1)}), (bf16[2,128,640]{1,2,0:T(8,128)(2,1)}, ...) | async-done | bytes 1310736 | tf_op jit(solution)/shard_map/psum | solution.py:19
  386.6 1.9 fusion.322
  389.6 1.9 fusion.324
  392.8 1.8 copy.149
  401.2 1.4 fusion.38
  402.6 1.4 fusion.39
  404.1 1.4 fusion.40
  405.5 1.4 fusion.41
  407.0 1.4 fusion.42
  408.5 1.4 fusion.43
  409.9 1.4 fusion.44
  411.4 1.4 fusion.45
  412.8 1.6 fusion.46
  422.0 1.1 fusion.132
  424.3 1.1 fusion.136
  437.1 1.1 copy.206
  440.1 4.4 collective-permute-start.27
  444.5 1.9 copy.204
  448.5 1.9 collective-permute-start.26
  450.4 4.7 collective-permute-start.25
  455.1 1.9 copy.202
  459.1 1.3 collective-permute-start.24
  460.4 1.6 collective-permute-start.23
  470.6 1.3 pad_maximum_fusion
  475.1 1.3 collective-permute-start.22
  476.5 1.3 collective-permute-start.21
  477.8 11.3 %collective-permute-start.20 = (bf16[2,128,640]{1,2,0:T(8,128)(2,1)S(1)}, bf16[2,128,640]{1,2,0:T(8,128)(2,1)S(1)}, u32[]{:S(2)}, u32[]{:S(2)}) collective-permute-start(bf16[2,128,640]{1,2,0:T(8,128)(2,1)S(1)} %copy-done.53), channel_id=1, source_target_pairs={{28,0},{32,4},{36,8},{40,12},{44,16},{48,20},{52,24},{56,28},{60,3... | collective-permute-start | bytes 983048 | tf_op jit(solution)/shard_map/ppermute | solution.py:14
  489.1 1.9 collective-permute-start.19
  492.8 1.9 collective-permute-start.18
  495.4 5.3 collective-permute-start.17
  500.7 4.2 collective-permute-start.16
  505.0 6.5 collective-permute-start.15
  511.5 12.6 %collective-permute-start.14 = (bf16[2,128,640]{1,2,0:T(8,128)(2,1)}, bf16[2,128,640]{1,2,0:T(8,128)(2,1)}, u32[]{:S(2)}, u32[]{:S(2)}) collective-permute-start(bf16[2,128,640]{1,2,0:T(8,128)(2,1)} %fusion.70), channel_id=1, source_target_pairs={{4,0},{8,4},{12,8},{16,12},{20,16},{24,20},{28,24},{32,28},{36,32}... | collective-permute-start | bytes 983048 | tf_op jit(solution)/shard_map/ppermute | solution.py:14
  526.3 7.6 collective-permute-done.15
  533.9 296.4 %all-reduce.4.cloned.1.call-done = bf16[4,2,128,640]{2,3,1,0:T(8,128)(2,1)} async-done(((bf16[4,2,128,640]{2,3,1,0:T(8,128)(2,1)}), bf16[4,2,128,640]{2,3,1,0:T(8,128)(2,1)}) %all-reduce.4.cloned.1.call-update) | async-done | bytes 1310736 | tf_op jit(solution)/shard_map/psum | solution.py:145
  830.3 2.9 fusion.89
  (347 shorter events, 74.0 us)
Async XLA Ops:
  7.2 379.4 %all-reduce.6.cloned.1.call-start = ((), (), s32[]{:S(2)}) async-start(), calls=%async_computation.1 | async-start | bytes 2621440 | tf_op jit(solution)/shard_map/psum | solution.py:19
  13.9 25.2 %copy-start.61 = (s32[32]{0:T(128)S(1)}, s32[32]{0:T(128)}, u32[]{:S(2)}) copy-start(s32[32]{0:T(128)} %param.11) | copy-start | bytes 388
  13.9 27.1 %copy-start.79 = (bf16[128,640]{1,0:T(8,128)(2,1)S(1)}, bf16[128,640]{1,0:T(8,128)(2,1)}, u32[]{:S(2)}) copy-start(bf16[128,640]{1,0:T(8,128)(2,1)} %param.10) | copy-start | bytes 491524
  15.2 26.0 %copy-start.80 = (bf16[128,640]{1,0:T(8,128)(2,1)S(1)}, bf16[128,640]{1,0:T(8,128)(2,1)}, u32[]{:S(2)}) copy-start(bf16[128,640]{1,0:T(8,128)(2,1)} %param.7) | copy-start | bytes 491524
  15.2 61.1 %collective-permute-start.13 = (bf16[2,128,640]{1,2,0:T(8,128)(2,1)}, bf16[2,128,640]{1,2,0:T(8,128)(2,1)S(1)}, u32[]{:S(2)}, u32[]{:S(2)}) collective-permute-start(bf16[2,128,640]{1,2,0:T(8,128)(2,1)} %get-tuple-element.96), channel_id=1, source_target_pairs={{12,0},{16,4},{20,8},{24,12},{28,16},{32,20},{36,24},{40,28},{44,3... | collective-permute-start | bytes 983048 | tf_op jit(solution)/shard_map/ppermute | solution.py:14
  18.5 60.3 %collective-permute-start.12 = (bf16[2,128,640]{1,2,0:T(8,128)(2,1)}, bf16[2,128,640]{1,2,0:T(8,128)(2,1)S(1)}, u32[]{:S(2)}, u32[]{:S(2)}) collective-permute-start(bf16[2,128,640]{1,2,0:T(8,128)(2,1)} %get-tuple-element.96), channel_id=1, source_target_pairs={{8,0},{12,4},{16,8},{20,12},{24,16},{28,20},{32,24},{36,28},{40,32... | collective-permute-start | bytes 983048 | tf_op jit(solution)/shard_map/ppermute | solution.py:14
  20.5 60.3 %collective-permute-start.11 = (bf16[2,128,640]{1,2,0:T(8,128)(2,1)}, bf16[2,128,640]{1,2,0:T(8,128)(2,1)S(1)}, u32[]{:S(2)}, u32[]{:S(2)}) collective-permute-start(bf16[2,128,640]{1,2,0:T(8,128)(2,1)} %get-tuple-element.96), channel_id=1, source_target_pairs={{4,0},{8,4},{12,8},{16,12},{20,16},{24,20},{28,24},{32,28},{36,32}... | collective-permute-start | bytes 983048 | tf_op jit(solution)/shard_map/ppermute | solution.py:14
  24.6 58.8 %collective-permute-start.10 = (bf16[2,128,640]{1,2,0:T(8,128)(2,1)}, bf16[2,128,640]{1,2,0:T(8,128)(2,1)S(1)}, u32[]{:S(2)}, u32[]{:S(2)}) collective-permute-start(bf16[2,128,640]{1,2,0:T(8,128)(2,1)} %get-tuple-element.96), channel_id=1, source_target_pairs={{0,44},{4,48},{8,52},{12,56},{16,60},{20,64},{24,68},{28,72},{32,7... | collective-permute-start | bytes 983048 | tf_op jit(solution)/shard_map/ppermute | solution.py:14
  33.9 52.1 %collective-permute-start.9 = (bf16[2,128,640]{1,2,0:T(8,128)(2,1)}, bf16[2,128,640]{1,2,0:T(8,128)(2,1)S(1)}, u32[]{:S(2)}, u32[]{:S(2)}) collective-permute-start(bf16[2,128,640]{1,2,0:T(8,128)(2,1)} %get-tuple-element.96), channel_id=1, source_target_pairs={{0,40},{4,44},{8,48},{12,52},{16,56},{20,60},{24,64},{28,68},{32,7... | collective-permute-start | bytes 983048 | tf_op jit(solution)/shard_map/ppermute | solution.py:14
  39.0 25.9 %copy-start.82 = (s32[5]{0:T(128)S(1)}, s32[5]{0:T(128)}, u32[]{:S(2)}) copy-start(s32[5]{0:T(128)} %param.13) | copy-start | bytes 64
  39.1 791.2 %all-reduce.4.cloned.1.call-start = ((), (), s32[]{:S(2)}) async-start(), calls=%async_computation | async-start | bytes 2621440 | tf_op jit(solution)/shard_map/psum | solution.py:145
  76.3 12.9 %collective-permute-start.8 = (bf16[2,128,640]{1,2,0:T(8,128)(2,1)}, bf16[2,128,640]{1,2,0:T(8,128)(2,1)S(1)}, u32[]{:S(2)}, u32[]{:S(2)}) collective-permute-start(bf16[2,128,640]{1,2,0:T(8,128)(2,1)} %get-tuple-element.96), channel_id=1, source_target_pairs={{0,36},{4,40},{8,44},{12,48},{16,52},{20,56},{24,60},{28,64},{32,6... | collective-permute-start | bytes 983048 | tf_op jit(solution)/shard_map/ppermute | solution.py:14
  78.8 27.2 %collective-permute-start.7 = (bf16[2,128,640]{1,2,0:T(8,128)(2,1)}, bf16[2,128,640]{1,2,0:T(8,128)(2,1)S(1)}, u32[]{:S(2)}, u32[]{:S(2)}) collective-permute-start(bf16[2,128,640]{1,2,0:T(8,128)(2,1)} %get-tuple-element.96), channel_id=1, source_target_pairs={{0,32},{4,36},{8,40},{12,44},{16,48},{20,52},{24,56},{28,60},{32,6... | collective-permute-start | bytes 983048 | tf_op jit(solution)/shard_map/ppermute | solution.py:14
  80.8 30.4 %collective-permute-start.6 = (bf16[2,128,640]{1,2,0:T(8,128)(2,1)}, bf16[2,128,640]{1,2,0:T(8,128)(2,1)S(1)}, u32[]{:S(2)}, u32[]{:S(2)}) collective-permute-start(bf16[2,128,640]{1,2,0:T(8,128)(2,1)} %get-tuple-element.96), channel_id=1, source_target_pairs={{0,28},{4,32},{8,36},{12,40},{16,44},{20,48},{24,52},{28,56},{32,6... | collective-permute-start | bytes 983048 | tf_op jit(solution)/shard_map/ppermute | solution.py:14
  83.4 35.0 %collective-permute-start.5 = (bf16[2,128,640]{1,2,0:T(8,128)(2,1)}, bf16[2,128,640]{1,2,0:T(8,128)(2,1)S(1)}, u32[]{:S(2)}, u32[]{:S(2)}) collective-permute-start(bf16[2,128,640]{1,2,0:T(8,128)(2,1)} %get-tuple-element.96), channel_id=1, source_target_pairs={{0,24},{4,28},{8,32},{12,36},{16,40},{20,44},{24,48},{28,52},{32,5... | collective-permute-start | bytes 983048 | tf_op jit(solution)/shard_map/ppermute | solution.py:14
  86.0 35.1 %collective-permute-start.4 = (bf16[2,128,640]{1,2,0:T(8,128)(2,1)}, bf16[2,128,640]{1,2,0:T(8,128)(2,1)S(1)}, u32[]{:S(2)}, u32[]{:S(2)}) collective-permute-start(bf16[2,128,640]{1,2,0:T(8,128)(2,1)} %get-tuple-element.96), channel_id=1, source_target_pairs={{0,20},{4,24},{8,28},{12,32},{16,36},{20,40},{24,44},{28,48},{32,5... | collective-permute-start | bytes 983048 | tf_op jit(solution)/shard_map/ppermute | solution.py:14
  89.2 38.5 %collective-permute-start.3 = (bf16[2,128,640]{1,2,0:T(8,128)(2,1)}, bf16[2,128,640]{1,2,0:T(8,128)(2,1)S(1)}, u32[]{:S(2)}, u32[]{:S(2)}) collective-permute-start(bf16[2,128,640]{1,2,0:T(8,128)(2,1)} %get-tuple-element.96), channel_id=1, source_target_pairs={{0,16},{4,20},{8,24},{12,28},{16,32},{20,36},{24,40},{28,44},{32,4... | collective-permute-start | bytes 983048 | tf_op jit(solution)/shard_map/ppermute | solution.py:14
  106.0 23.0 %collective-permute-start.2 = (bf16[2,128,640]{1,2,0:T(8,128)(2,1)}, bf16[2,128,640]{1,2,0:T(8,128)(2,1)}, u32[]{:S(2)}, u32[]{:S(2)}) collective-permute-start(bf16[2,128,640]{1,2,0:T(8,128)(2,1)} %get-tuple-element.96), channel_id=1, source_target_pairs={{0,12},{4,16},{8,20},{12,24},{16,28},{20,32},{24,36},{28,40},{32,4... | collective-permute-start | bytes 983048 | tf_op jit(solution)/shard_map/ppermute | solution.py:14
  111.2 23.2 %collective-permute-start.1 = (bf16[2,128,640]{1,2,0:T(8,128)(2,1)}, bf16[2,128,640]{1,2,0:T(8,128)(2,1)}, u32[]{:S(2)}, u32[]{:S(2)}) collective-permute-start(bf16[2,128,640]{1,2,0:T(8,128)(2,1)} %get-tuple-element.96), channel_id=1, source_target_pairs={{0,8},{4,12},{8,16},{12,20},{16,24},{20,28},{24,32},{28,36},{32,40... | collective-permute-start | bytes 983048 | tf_op jit(solution)/shard_map/ppermute | solution.py:14
  118.4 23.1 %collective-permute-start = (bf16[2,128,640]{1,2,0:T(8,128)(2,1)}, bf16[2,128,640]{1,2,0:T(8,128)(2,1)}, u32[]{:S(2)}, u32[]{:S(2)}) collective-permute-start(bf16[2,128,640]{1,2,0:T(8,128)(2,1)} %get-tuple-element.96), channel_id=1, source_target_pairs={{0,4},{4,8},{8,12},{12,16},{16,20},{20,24},{24,28},{28,32},{32,36}... | collective-permute-start | bytes 983048 | tf_op jit(solution)/shard_map/ppermute | solution.py:14
  131.0 5.3 copy-start.20
  131.1 5.3 copy-start.22
  136.3 7.7 copy-start.25
  136.5 7.7 copy-start.27
  137.6 7.1 copy-start.42
  144.2 3.2 copy-start.29
  144.3 3.0 copy-start.31
  144.5 2.8 copy-start.33
  144.7 3.8 copy-start.35
  144.9 3.6 copy-start.37
  146.2 3.4 copy-start.48
  391.7 4.2 copy-start.12
  392.8 3.1 copy-start.14
  416.2 14.4 %copy-start.9 = (bf16[5,256,128]{2,1,0:T(8,128)(2,1)}, bf16[5,256,128]{2,1,0:T(8,128)(2,1)S(1)}, u32[]{:S(2)}) copy-start(bf16[5,256,128]{2,1,0:T(8,128)(2,1)S(1)} %fusion.19) | copy-start | bytes 983044
  419.7 48.7 %copy-start.6 = (bf16[5,128,128]{2,1,0:T(8,128)(2,1)}, bf16[5,128,128]{2,1,0:T(8,128)(2,1)S(1)}, u32[]{:S(2)}) copy-start(bf16[5,128,128]{2,1,0:T(8,128)(2,1)S(1)} %fusion.50) | copy-start | bytes 491524
  440.1 35.0 %collective-permute-start.27 = (bf16[2,128,640]{1,2,0:T(8,128)(2,1)}, bf16[2,128,640]{1,2,0:T(8,128)(2,1)}, u32[]{:S(2)}, u32[]{:S(2)}) collective-permute-start(bf16[2,128,640]{1,2,0:T(8,128)(2,1)} %get-tuple-element.41), channel_id=1, source_target_pairs={{0,12},{4,16},{8,20},{12,24},{16,28},{20,32},{24,36},{28,40},{32,4... | collective-permute-start | bytes 983048 | tf_op jit(solution)/shard_map/ppermute | solution.py:14
  448.5 28.0 %collective-permute-start.26 = (bf16[2,128,640]{1,2,0:T(8,128)(2,1)}, bf16[2,128,640]{1,2,0:T(8,128)(2,1)}, u32[]{:S(2)}, u32[]{:S(2)}) collective-permute-start(bf16[2,128,640]{1,2,0:T(8,128)(2,1)} %get-tuple-element.55), channel_id=1, source_target_pairs={{0,8},{4,12},{8,16},{12,20},{16,24},{20,28},{24,32},{28,36},{32,40... | collective-permute-start | bytes 983048 | tf_op jit(solution)/shard_map/ppermute | solution.py:14
  450.4 27.4 %collective-permute-start.25 = (bf16[2,128,640]{1,2,0:T(8,128)(2,1)}, bf16[2,128,640]{1,2,0:T(8,128)(2,1)}, u32[]{:S(2)}, u32[]{:S(2)}) collective-permute-start(bf16[2,128,640]{1,2,0:T(8,128)(2,1)} %get-tuple-element.54), channel_id=1, source_target_pairs={{0,4},{4,8},{8,12},{12,16},{16,20},{20,24},{24,28},{28,32},{32,36}... | collective-permute-start | bytes 983048 | tf_op jit(solution)/shard_map/ppermute | solution.py:14
  459.1 30.0 %collective-permute-start.24 = (bf16[2,128,640]{1,2,0:T(8,128)(2,1)}, bf16[2,128,640]{1,2,0:T(8,128)(2,1)}, u32[]{:S(2)}, u32[]{:S(2)}) collective-permute-start(bf16[2,128,640]{1,2,0:T(8,128)(2,1)} %get-tuple-element.53), channel_id=1, source_target_pairs={{44,0},{48,4},{52,8},{56,12},{60,16},{64,20},{68,24},{72,28},{76,3... | collective-permute-start | bytes 983048 | tf_op jit(solution)/shard_map/ppermute | solution.py:14
  460.4 32.4 %collective-permute-start.23 = (bf16[2,128,640]{1,2,0:T(8,128)(2,1)}, bf16[2,128,640]{1,2,0:T(8,128)(2,1)}, u32[]{:S(2)}, u32[]{:S(2)}) collective-permute-start(bf16[2,128,640]{1,2,0:T(8,128)(2,1)} %get-tuple-element.52), channel_id=1, source_target_pairs={{40,0},{44,4},{48,8},{52,12},{56,16},{60,20},{64,24},{68,28},{72,3... | collective-permute-start | bytes 983048 | tf_op jit(solution)/shard_map/ppermute | solution.py:14
  473.5 2.9 copy-start.52
  473.6 4.2 copy-start.53
  473.6 15.5 %copy-start.51 = (bf16[2,128,640]{1,2,0:T(8,128)(2,1)S(1)}, bf16[2,128,640]{1,2,0:T(8,128)(2,1)}, u32[]{:S(2)}) copy-start(bf16[2,128,640]{1,2,0:T(8,128)(2,1)} %get-tuple-element.48) | copy-start | bytes 983044
  475.1 20.3 %collective-permute-start.22 = (bf16[2,128,640]{1,2,0:T(8,128)(2,1)S(1)}, bf16[2,128,640]{1,2,0:T(8,128)(2,1)S(1)}, u32[]{:S(2)}, u32[]{:S(2)}) collective-permute-start(bf16[2,128,640]{1,2,0:T(8,128)(2,1)S(1)} %copy-done.54), channel_id=1, source_target_pairs={{36,0},{40,4},{44,8},{48,12},{52,16},{56,20},{60,24},{64,28},{68,3... | collective-permute-start | bytes 983048 | tf_op jit(solution)/shard_map/ppermute | solution.py:14
  476.5 24.3 %collective-permute-start.21 = (bf16[2,128,640]{1,2,0:T(8,128)(2,1)S(1)}, bf16[2,128,640]{1,2,0:T(8,128)(2,1)S(1)}, u32[]{:S(2)}, u32[]{:S(2)}) collective-permute-start(bf16[2,128,640]{1,2,0:T(8,128)(2,1)S(1)} %copy-done.52), channel_id=1, source_target_pairs={{32,0},{36,4},{40,8},{44,12},{48,16},{52,20},{56,24},{60,28},{64,3... | collective-permute-start | bytes 983048 | tf_op jit(solution)/shard_map/ppermute | solution.py:14
  477.8 27.2 %collective-permute-start.20 = (bf16[2,128,640]{1,2,0:T(8,128)(2,1)S(1)}, bf16[2,128,640]{1,2,0:T(8,128)(2,1)S(1)}, u32[]{:S(2)}, u32[]{:S(2)}) collective-permute-start(bf16[2,128,640]{1,2,0:T(8,128)(2,1)S(1)} %copy-done.53), channel_id=1, source_target_pairs={{28,0},{32,4},{36,8},{40,12},{44,16},{48,20},{52,24},{56,28},{60,3... | collective-permute-start | bytes 983048 | tf_op jit(solution)/shard_map/ppermute | solution.py:14
  489.1 22.4 %collective-permute-start.19 = (bf16[2,128,640]{1,2,0:T(8,128)(2,1)S(1)}, bf16[2,128,640]{1,2,0:T(8,128)(2,1)S(1)}, u32[]{:S(2)}, u32[]{:S(2)}) collective-permute-start(bf16[2,128,640]{1,2,0:T(8,128)(2,1)S(1)} %copy-done.51), channel_id=1, source_target_pairs={{24,0},{28,4},{32,8},{36,12},{40,16},{44,20},{48,24},{52,28},{56,3... | collective-permute-start | bytes 983048 | tf_op jit(solution)/shard_map/ppermute | solution.py:14
  491.0 4.4 copy-start.50
  491.0 33.0 %copy-start.13 = (bf16[128,5,128]{2,0,1:T(8,128)(2,1)S(1)}, bf16[128,5,128]{2,0,1:T(8,128)(2,1)}, u32[]{:S(2)}) copy-start(bf16[128,5,128]{2,0,1:T(8,128)(2,1)} %copy-done.12) | copy-start | bytes 491524
  491.0 33.0 %copy-start.15 = (bf16[128,5,128]{2,0,1:T(8,128)(2,1)S(1)}, bf16[128,5,128]{2,0,1:T(8,128)(2,1)}, u32[]{:S(2)}) copy-start(bf16[128,5,128]{2,0,1:T(8,128)(2,1)} %copy-done.14) | copy-start | bytes 491524
  491.8 32.6 %copy-start.81 = (bf16[128,5,128]{0,2,1:T(8,128)(2,1)S(1)}, bf16[128,5,128]{0,2,1:T(8,128)(2,1)}, u32[]{:S(2)}) copy-start(bf16[128,5,128]{0,2,1:T(8,128)(2,1)} %get-tuple-element.159) | copy-start | bytes 491524
  491.8 33.5 %copy-start.5 = (bf16[1,128,640]{1,2,0:T(8,128)(2,1)S(1)}, bf16[1,128,640]{1,2,0:T(8,128)(2,1)}, u32[]{:S(2)}) copy-start(bf16[1,128,640]{1,2,0:T(8,128)(2,1)} %copy-done.4) | copy-start | bytes 491524
  491.8 33.5 %copy-start.7 = (bf16[5,128,128]{2,1,0:T(8,128)(2,1)S(1)}, bf16[5,128,128]{2,1,0:T(8,128)(2,1)}, u32[]{:S(2)}) copy-start(bf16[5,128,128]{2,1,0:T(8,128)(2,1)} %copy-done.6) | copy-start | bytes 491524
  492.8 33.5 %collective-permute-start.18 = (bf16[2,128,640]{1,2,0:T(8,128)(2,1)}, bf16[2,128,640]{1,2,0:T(8,128)(2,1)}, u32[]{:S(2)}, u32[]{:S(2)}) collective-permute-start(bf16[2,128,640]{1,2,0:T(8,128)(2,1)} %get-tuple-element.47), channel_id=1, source_target_pairs={{20,0},{24,4},{28,8},{32,12},{36,16},{40,20},{44,24},{48,28},{52,3... | collective-permute-start | bytes 983048 | tf_op jit(solution)/shard_map/ppermute | solution.py:14
  495.4 29.0 %copy-start.55 = (bf16[2,128,640]{1,2,0:T(8,128)(2,1)}, bf16[2,128,640]{1,2,0:T(8,128)(2,1)S(1)}, u32[]{:S(2)}) copy-start(bf16[2,128,640]{1,2,0:T(8,128)(2,1)S(1)} %collective-permute-done.22) | copy-start | bytes 983044
  495.4 30.9 %collective-permute-start.17 = (bf16[2,128,640]{1,2,0:T(8,128)(2,1)S(1)}, bf16[2,128,640]{1,2,0:T(8,128)(2,1)}, u32[]{:S(2)}, u32[]{:S(2)}) collective-permute-start(bf16[2,128,640]{1,2,0:T(8,128)(2,1)S(1)} %copy-done.50), channel_id=1, source_target_pairs={{16,0},{20,4},{24,8},{28,12},{32,16},{36,20},{40,24},{44,28},{48,3... | collective-permute-start | bytes 983048 | tf_op jit(solution)/shard_map/ppermute | solution.py:14
  500.7 23.7 %copy-start.57 = (bf16[2,128,640]{1,2,0:T(8,128)(2,1)}, bf16[2,128,640]{1,2,0:T(8,128)(2,1)S(1)}, u32[]{:S(2)}) copy-start(bf16[2,128,640]{1,2,0:T(8,128)(2,1)S(1)} %collective-permute-done.21) | copy-start | bytes 983044
  500.7 25.6 %collective-permute-start.16 = (bf16[2,128,640]{1,2,0:T(8,128)(2,1)}, bf16[2,128,640]{1,2,0:T(8,128)(2,1)}, u32[]{:S(2)}, u32[]{:S(2)}) collective-permute-start(bf16[2,128,640]{1,2,0:T(8,128)(2,1)} %get-tuple-element.45), channel_id=1, source_target_pairs={{12,0},{16,4},{20,8},{24,12},{28,16},{32,20},{36,24},{40,28},{44,3... | collective-permute-start | bytes 983048 | tf_op jit(solution)/shard_map/ppermute | solution.py:14
  505.0 19.5 %copy-start.59 = (bf16[2,128,640]{1,2,0:T(8,128)(2,1)}, bf16[2,128,640]{1,2,0:T(8,128)(2,1)S(1)}, u32[]{:S(2)}) copy-start(bf16[2,128,640]{1,2,0:T(8,128)(2,1)S(1)} %collective-permute-done.20) | copy-start | bytes 983044
  505.0 28.9 %collective-permute-start.15 = (bf16[2,128,640]{1,2,0:T(8,128)(2,1)}, bf16[2,128,640]{1,2,0:T(8,128)(2,1)}, u32[]{:S(2)}, u32[]{:S(2)}) collective-permute-start(bf16[2,128,640]{1,2,0:T(8,128)(2,1)} %get-tuple-element.44), channel_id=1, source_target_pairs={{8,0},{12,4},{16,8},{20,12},{24,16},{28,20},{32,24},{36,28},{40,32... | collective-permute-start | bytes 983048 | tf_op jit(solution)/shard_map/ppermute | solution.py:14
  511.5 12.9 %copy-start.60 = (bf16[2,128,640]{1,2,0:T(8,128)(2,1)}, bf16[2,128,640]{1,2,0:T(8,128)(2,1)S(1)}, u32[]{:S(2)}) copy-start(bf16[2,128,640]{1,2,0:T(8,128)(2,1)S(1)} %collective-permute-done.19) | copy-start | bytes 983044
  511.5 22.4 %collective-permute-start.14 = (bf16[2,128,640]{1,2,0:T(8,128)(2,1)}, bf16[2,128,640]{1,2,0:T(8,128)(2,1)}, u32[]{:S(2)}, u32[]{:S(2)}) collective-permute-start(bf16[2,128,640]{1,2,0:T(8,128)(2,1)} %fusion.70), channel_id=1, source_target_pairs={{4,0},{8,4},{12,8},{16,12},{20,16},{24,20},{28,24},{32,28},{36,32}... | collective-permute-start | bytes 983048 | tf_op jit(solution)/shard_map/ppermute | solution.py:14
  524.4 305.9 %copy-start.56 = (bf16[2,128,640]{1,2,0:T(8,128)(2,1)S(1)}, bf16[2,128,640]{1,2,0:T(8,128)(2,1)}, u32[]{:S(2)}) copy-start(bf16[2,128,640]{1,2,0:T(8,128)(2,1)} %copy-done.55) | copy-start | bytes 983044
  524.4 305.9 %copy-start.58 = (bf16[2,128,640]{1,2,0:T(8,128)(2,1)S(1)}, bf16[2,128,640]{1,2,0:T(8,128)(2,1)}, u32[]{:S(2)}) copy-start(bf16[2,128,640]{1,2,0:T(8,128)(2,1)} %copy-done.57) | copy-start | bytes 983044
  (49 other events, 80.9 us)
Sparse Core Ops, SparseCore 0:
  39.2 347.3 all-reduce.5
  472.0 358.2 all-reduce.3
where the time goes:
time: 855 us; the launch traced here: 842 us
  waiting for transfers between devices  568 us (66%)
  starting transfers between devices  109 us (13%)
  local copies, waits for them, and re-layouts  50.1 us (6%)
  between operations  42.3 us (5%)
  matrix products  42.2 us (5%)
  other arithmetic  30.5 us (4%)
    psum x1, waiting for transfers between devices, per_device(): lax.psum(jnp.stack(partials[15:19]).astype(jnp.bfloat16), 'tm')  296 us
    psum x1, waiting for transfers between devices, broadcast(): return lax.psum(block, axis)  237 us
    ppermute x28, starting transfers between devices, passed_along(): return lax.ppermute(value, axis, pairs)  109 us
    ppermute x28, waiting for transfers between devices, passed_along(): return lax.ppermute(value, axis, pairs)  34.8 us
  transfers between devices with their start and end apart: 30, of which 9 were waited for; matrix products, arithmetic and copies ran while one was open for 7% of the time, Pallas kernels for 0%

commit v1 on v0

v1 whole, which is shorter than its diff:
```python
import math

import jax
import jax.numpy as jnp
from jax import lax
from jax.experimental import pallas as pl
from jax.experimental.pallas import tpu as pltpu
from jax.sharding import PartitionSpec as P

MESH = pl.DeviceIdType.MESH
BLK = 128
DH = 128
HPD = 5
RING = 4
PLANE = 8
NBLK = RING * PLANE
BF16 = jnp.bfloat16
F32 = jnp.float32
TILE_Q = 2 * BLK
MAX_CHUNKS = 5
NEG = -1e30


def position():
    tm = lax.axis_index("tm")
    head = lax.axis_index("head")
    return tm // PLANE, tm % PLANE, head // 2, head % 2


def owner_of(j, x_lo, core):
    first = (2 * (j % 4) + j // 4, 0)
    u = HPD + j
    second = (2 * (u % 4) + u // 4, 0) if u < 8 else ((0, 5)[u - 8], 1)
    place = first[0] + core * (second[0] - first[0])
    core_there = first[1] + core * (second[1] - first[1])
    return place, 2 * (1 - x_lo) + core_there


def my_task(place, x_lo, core):
    u_first = (place % 2) * 4 + place // 2
    u = (1 - core) * u_first + core * (8 + place // 5)
    is_owner = (core == 0) | (place == 0) | (place == 5)
    return is_owner, 2 * (1 - x_lo) + u // HPD, u % HPD


def gather_kernel(
    q_ref, k_ref, v_ref, do_ref, w_ref,
    qo_ref, doo_ref, kvo_ref, wo_ref,
    send_sem, w_send, qd_sem, kv_sem, w_sem, up_sem, down_sem, up2_sem, down2_sem, ring_send,
):
    y, place, x_lo, core = position()
    is_owner, src_head, _ = my_task(place, x_lo, core)
    me_head = lax.axis_index("head")
    up = lax.rem(y + 1, RING)
    down = lax.rem(y + RING - 1, RING)
    far = lax.rem(y + 2, RING)
    base = y * PLANE
    up_id = (up * PLANE + place, me_head)
    down_id = (down * PLANE + place, me_head)

    barrier = pltpu.get_barrier_semaphore()

    @pl.when(is_owner)
    def _():
        for r in range(PLANE):
            pl.semaphore_signal(
                barrier, inc=1, device_id=(base + r, src_head), device_id_type=MESH
            )
        pl.semaphore_signal(barrier, inc=1, device_id=up_id, device_id_type=MESH)
        pl.semaphore_signal(barrier, inc=1, device_id=down_id, device_id_type=MESH)
        pl.semaphore_wait(barrier, HPD + 2)

    @pl.when(jnp.logical_not(is_owner))
    def _():
        pl.semaphore_wait(barrier, HPD)

    def column(ref, j):
        return ref.at[:, pl.ds(j * DH, DH)]

    rows = pl.ds(pl.multiple_of(place * BLK, BLK), BLK)
    owners = [owner_of(j, x_lo, core) for j in range(HPD)]
    targets = [(base + there, head) for there, head in owners]
    for j in range(HPD):
        for part, ref in enumerate((k_ref, v_ref)):
            pltpu.make_async_remote_copy(
                src_ref=column(ref, j), dst_ref=kvo_ref.at[base + place, part],
                send_sem=send_sem.at[part], recv_sem=kv_sem.at[place],
                device_id=targets[j], device_id_type=MESH,
            ).start()
    for j in range(HPD):
        for part, (ref, out) in enumerate(((q_ref, qo_ref), (do_ref, doo_ref))):
            pltpu.make_async_remote_copy(
                src_ref=column(ref, j), dst_ref=out.at[rows],
                send_sem=send_sem.at[2 + part], recv_sem=qd_sem.at[part],
                device_id=targets[j], device_id_type=MESH,
            ).start()

    @pl.when(place == 0)
    def _():
        for j in range(HPD):
            pltpu.make_async_remote_copy(
                src_ref=w_ref.at[j], dst_ref=wo_ref, send_sem=w_send, recv_sem=w_sem,
                device_id=targets[j], device_id_type=MESH,
            ).start()

    @pl.when(is_owner)
    def _():
        def pass_on(block, to, recv, lane):
            pltpu.make_async_remote_copy(
                src_ref=kvo_ref.at[block], dst_ref=kvo_ref.at[block],
                send_sem=ring_send.at[lane], recv_sem=recv,
                device_id=to, device_id_type=MESH,
            ).start()

        def arrived(block, sem):
            pltpu.make_async_copy(kvo_ref.at[block], kvo_ref.at[block], sem).wait()

        for r in range(PLANE):
            arrived(base + r, kv_sem.at[r])
            pass_on(base + r, up_id, up_sem.at[r], 0)
            pass_on(base + r, down_id, down_sem.at[r], 1)
        half = PLANE // 2
        for r in range(half):
            arrived(down * PLANE + r, up_sem.at[r])
            pass_on(down * PLANE + r, up_id, up2_sem.at[r], 2)
            arrived(up * PLANE + half + r, down_sem.at[half + r])
            pass_on(up * PLANE + half + r, down_id, down2_sem.at[r], 3)
        for r in range(half):
            arrived(down * PLANE + half + r, up_sem.at[half + r])
            arrived(up * PLANE + r, down_sem.at[r])
        for r in range(half):
            arrived(far * PLANE + r, up2_sem.at[r])
            arrived(far * PLANE + half + r, down2_sem.at[r])
        pltpu.make_async_copy(qo_ref, qo_ref, qd_sem.at[0]).wait()
        pltpu.make_async_copy(doo_ref, doo_ref, qd_sem.at[1]).wait()
        pltpu.make_async_copy(wo_ref, wo_ref, w_sem).wait()
        for lane, count in enumerate((PLANE, PLANE, half, half)):
            some = kvo_ref.at[pl.ds(0, count)]
            pltpu.make_async_copy(some, some, ring_send.at[lane]).wait()

    for part, ref in enumerate((k_ref, v_ref, q_ref, do_ref)):
        pltpu.make_async_copy(ref, ref, send_sem.at[part]).wait()

    @pl.when(place == 0)
    def _():
        pltpu.make_async_copy(w_ref, w_ref, w_send).wait()


def attend_kernel(
    fid_ref, sink_ref, w_ref, q_ref, do_ref, kv_ref,
    att_ref, dq_ref, dkv_ref,
    t_s, p_s, dk_s, dv_s,
):
    y, place, x_lo, core = position()
    is_owner, _, _ = my_task(place, x_lo, core)
    scale = 1.0 / math.sqrt(DH)
    slope = scale * math.log2(math.e)
    chunk = 4 * BLK

    @pl.when(is_owner)
    def _():
        c = 1 + fid_ref[1] + fid_ref[2]
        sink = sink_ref[0]
        win = w_ref[0, 0]
        dk_s[...] = jnp.zeros_like(dk_s)
        dv_s[...] = jnp.zeros_like(dv_s)
        lane = lax.broadcasted_iota(jnp.int32, (1, TILE_Q), 1)

        def sees(query_frame, frame):
            near = (frame <= query_frame) & (frame > query_frame - win)
            return near | ((frame == sink) & (sink <= query_frame))

        @pl.loop(0, PLANE // 2)
        def _(t):
            rows = pl.ds(pl.multiple_of(t * TILE_Q, TILE_Q), TILE_Q)
            block_a = y * PLANE + 2 * t
            frame_a = (block_a + c) // 4
            frame_b = (block_a + 1 + c) // 4
            low = jnp.maximum(frame_a - win + 1, 0)
            near_count = frame_b - low + 1
            count = near_count + (sink < low).astype(jnp.int32)

            def frame_at(i):
                return jnp.where(i < near_count, low + i, sink)

            def start_of(frame):
                return jnp.clip(4 * frame - c, 0, NBLK - 4)

            q_tile = q_ref[rows]
            q_t = q_tile.T

            def scores(i, top):
                frame = frame_at(i)
                start = start_of(frame)
                see_a = sees(frame_a, frame)
                see_b = sees(frame_b, frame)
                keys = kv_ref[pl.ds(start, 4), 0].reshape(chunk, DH)
                s = jnp.dot(keys, q_t, preferred_element_type=F32)
                for k in range(4):
                    here = (start + k + c) // 4 == frame
                    bias = jnp.where(
                        lane < BLK,
                        jnp.where(here & see_a, 0.0, NEG),
                        jnp.where(here & see_b, 0.0, NEG),
                    )
                    part = s[k * BLK : (k + 1) * BLK] + bias
                    t_s[pl.ds(i * chunk + k * BLK, BLK), :] = part
                    top = jnp.maximum(top, jnp.max(part.reshape(BLK // 8, 8, TILE_Q), axis=0))
                return top

            top = lax.fori_loop(0, count, scores, jnp.full((8, TILE_Q), NEG, F32))
            top = jnp.max(top, axis=0, keepdims=True) * slope

            def mix(i, carry):
                total, mixed = carry
                start = start_of(frame_at(i))
                at = pl.ds(pl.multiple_of(i * chunk, chunk), chunk)
                p = jnp.exp2(t_s[at, :] * slope - top)
                total = total + jnp.sum(p.reshape(chunk // 8, 8, TILE_Q), axis=0)
                p = p.astype(BF16)
                p_s[at, :] = p
                values = kv_ref[pl.ds(start, 4), 1].reshape(chunk, DH)
                mixed = mixed + lax.dot_general(
                    values, p, (((0,), (0,)), ((), ())), preferred_element_type=F32
                )
                return total, mixed

            total, mixed = lax.fori_loop(
                0, count, mix, (jnp.zeros((8, TILE_Q), F32), jnp.zeros((DH, TILE_Q), F32))
            )
            inverse = 1.0 / jnp.sum(total, axis=0, keepdims=True)
            att_t = (mixed * inverse).astype(BF16)
            att_ref[rows] = att_t.T
            do_t = (do_ref[rows].T.astype(F32) * inverse).astype(BF16)
            do_n = do_t.T
            delta = jnp.sum(do_t.astype(F32) * att_t.astype(F32), axis=0, keepdims=True)

            def back(i, dq_t):
                start = start_of(frame_at(i))
                at = pl.ds(pl.multiple_of(i * chunk, chunk), chunk)
                keys = kv_ref[pl.ds(start, 4), 0].reshape(chunk, DH)
                values = kv_ref[pl.ds(start, 4), 1].reshape(chunk, DH)
                p = p_s[at, :]
                dp = jnp.dot(values, do_t, preferred_element_type=F32)
                g = (p.astype(F32) * (dp - delta)).astype(BF16)
                dk = jnp.dot(g, q_tile, preferred_element_type=F32)
                dv = jnp.dot(p, do_n, preferred_element_type=F32)
                dk_s[pl.ds(start, 4)] += dk.reshape(4, BLK, DH)
                dv_s[pl.ds(start, 4)] += dv.reshape(4, BLK, DH)
                return dq_t + lax.dot_general(
                    keys, g, (((0,), (0,)), ((), ())), preferred_element_type=F32
                )

            dq_t = lax.fori_loop(0, count, back, jnp.zeros((DH, TILE_Q), F32))
            dq_ref[rows] = (dq_t * scale).astype(BF16).T

        @pl.loop(0, NBLK)
        def _(b):
            dkv_ref[b, 0] = (dk_s[b] * scale).astype(BF16)
            dkv_ref[b, 1] = dv_s[b].astype(BF16)


def scatter_kernel(
    att_ref, dq_ref, dkv_ref,
    atto_ref, dqo_ref, dko_ref, dvo_ref,
    got, acc, done, own_sem, out_sem, in_sem, part_send, part_sem, done_send, keep,
):
    y, place, x_lo, core = position()
    is_owner, src_head, j_there = my_task(place, x_lo, core)
    me_head = lax.axis_index("head")
    base = y * PLANE
    owners = [owner_of(j, x_lo, core) for j in range(HPD)]
    column = pl.ds(pl.multiple_of(j_there * DH, DH), DH)

    barrier = pltpu.get_barrier_semaphore()
    for there, head in owners:
        pl.semaphore_signal(barrier, inc=1, device_id=(base + there, head), device_id_type=MESH)

    @pl.when(is_owner)
    def _():
        planes = [lax.rem(y + d, RING) for d in range(RING)]
        for d in range(1, RING):
            pl.semaphore_signal(
                barrier, inc=1, device_id=(planes[d] * PLANE + place, me_head),
                device_id_type=MESH,
            )
        mine = pltpu.make_async_copy(dkv_ref.at[pl.ds(base, PLANE)], keep, own_sem)
        mine.start()
        pl.semaphore_wait(barrier, PLANE + RING - 1)

        def part_copy(d, r):
            return pltpu.make_async_remote_copy(
                src_ref=dkv_ref.at[planes[d] * PLANE + r], dst_ref=got.at[d - 1, r],
                send_sem=part_send.at[d - 1], recv_sem=part_sem.at[d - 1, r],
                device_id=(planes[d] * PLANE + place, me_head), device_id_type=MESH,
            )

        def sent_when(d):
            return y + d >= RING

        def got_when(d):
            return y < d

        for r in range(PLANE):
            for d in (2, 1, 3):
                if d == 1 and r < 3:
                    part_copy(d, r).start()
                else:
                    pl.when(sent_when(d))(lambda d=d, r=r: part_copy(d, r).start())
        for r in range(PLANE):
            for part, (ref, out) in enumerate(((att_ref, atto_ref), (dq_ref, dqo_ref))):
                pltpu.make_async_remote_copy(
                    src_ref=ref.at[pl.ds(r * BLK, BLK)], dst_ref=out.at[:, column],
                    send_sem=out_sem.at[part], recv_sem=in_sem.at[part],
                    device_id=(base + r, src_head), device_id_type=MESH,
                ).start()
        mine.wait()
        for r in range(PLANE):
            acc[...] = keep[r].astype(F32)

            def add(d, r=r):
                pltpu.make_async_copy(got.at[d - 1, r], got.at[d - 1, r], part_sem.at[d - 1, r]).wait()
                acc[...] += got[d - 1, r].astype(F32)

            for d in (1, 3, 2):
                if d == 1 and r < 3:
                    add(d)
                else:
                    pl.when(got_when(d))(lambda d=d: add(d))
            done[r] = acc[...].astype(BF16)
            for part, out in enumerate((dko_ref, dvo_ref)):
                pltpu.make_async_remote_copy(
                    src_ref=done.at[r, part], dst_ref=out.at[:, column],
                    send_sem=done_send, recv_sem=in_sem.at[2 + part],
                    device_id=(base + r, src_head), device_id_type=MESH,
                ).start()
        for part, ref in enumerate((att_ref, dq_ref)):
            pltpu.make_async_copy(ref, ref, out_sem.at[part]).wait()
        pltpu.make_async_copy(done, done, done_send).wait()

        def drained(d, count):
            some = dkv_ref.at[pl.ds(0, count)]
            pltpu.make_async_copy(some, some, part_send.at[d - 1]).wait()

        pl.when(sent_when(1))(lambda: drained(1, PLANE))
        pl.when(jnp.logical_not(sent_when(1)))(lambda: drained(1, 3))
        pl.when(sent_when(2))(lambda: drained(2, PLANE))
        pl.when(sent_when(3))(lambda: drained(3, PLANE))

    for part, ref in enumerate((atto_ref, dqo_ref, dko_ref, dvo_ref)):
        pltpu.make_async_copy(ref, ref, in_sem.at[part]).wait()


def per_device(query, key, value, grad_out, frame_ids, sink_frame, window):
    any_spec = pl.BlockSpec(memory_space=pl.ANY)
    smem = pl.BlockSpec(memory_space=pltpu.SMEM)
    vmem = pl.BlockSpec(memory_space=pltpu.VMEM)
    dma = pltpu.SemaphoreType.DMA
    shape = jax.ShapeDtypeStruct
    rows = PLANE * BLK
    windows = jnp.broadcast_to(window[:, None, None], (HPD, 8, 128))
    q_all, do_all, kv_all, w_all = pl.pallas_call(
        gather_kernel,
        out_shape=(
            shape((rows, DH), BF16),
            shape((rows, DH), BF16),
            shape((NBLK, 2, BLK, DH), BF16),
            shape((8, 128), jnp.int32),
        ),
        in_specs=[any_spec] * 5,
        out_specs=[any_spec] * 4,
        scratch_shapes=[
            dma((4,)), dma, dma((2,)), dma((PLANE,)), dma,
            dma((PLANE,)), dma((PLANE,)), dma((PLANE // 2,)), dma((PLANE // 2,)), dma((4,)),
        ],
        compiler_params=pltpu.CompilerParams(collective_id=0, has_side_effects=True),
        name="gather",
    )(query, key, value, grad_out, windows)
    att, dq, dkv = pl.pallas_call(
        attend_kernel,
        out_shape=(
            shape((rows, DH), BF16),
            shape((rows, DH), BF16),
            shape((NBLK, 2, BLK, DH), BF16),
        ),
        in_specs=[smem] * 3 + [vmem] * 3,
        out_specs=[vmem] * 3,
        scratch_shapes=[
            pltpu.VMEM((MAX_CHUNKS * 4 * BLK, TILE_Q), F32),
            pltpu.VMEM((MAX_CHUNKS * 4 * BLK, TILE_Q), BF16),
            pltpu.VMEM((NBLK, BLK, DH), F32),
            pltpu.VMEM((NBLK, BLK, DH), F32),
        ],
        name="attend",
    )(frame_ids, sink_frame, w_all, q_all, do_all, kv_all)
    return pl.pallas_call(
        scatter_kernel,
        out_shape=tuple(shape(query.shape, BF16) for _ in range(4)),
        in_specs=[any_spec] * 3,
        out_specs=[any_spec] * 4,
        scratch_shapes=[
            pltpu.VMEM((RING - 1, PLANE, 2, BLK, DH), BF16),
            pltpu.VMEM((2, BLK, DH), F32),
            pltpu.VMEM((PLANE, 2, BLK, DH), BF16),
            dma, dma((2,)), dma((4,)), dma((RING - 1,)), dma((RING - 1, PLANE)), dma,
            pltpu.VMEM((PLANE, 2, BLK, DH), BF16),
        ],
        compiler_params=pltpu.CompilerParams(collective_id=1, has_side_effects=True),
        name="scatter",
    )(att, dq, dkv)


def solution(mesh):
    tm_head = P("tm", "head")
    return jax.shard_map(
        per_device,
        mesh=mesh,
        in_specs=(tm_head, tm_head, tm_head, tm_head, P(), P(), P("head")),
        out_specs=(tm_head, tm_head, tm_head, tm_head),
        check_vma=False,
    )
```

time: 855 us -> 90.9 us (0.11); the launches traced: 842 us -> 89.8 us
  waiting for transfers between devices: 568 us -> 0 us
  starting transfers between devices: 109 us -> 0 us
  Pallas kernels: 0 us -> 80.8 us
  local copies, waits for them, and re-layouts: 50.1 us -> 7.72 us
  matrix products: 42.2 us -> 0 us
  between operations: 42.3 us -> 1.3 us
  other arithmetic: 30.5 us -> 0 us
    psum x2 -> x0, waiting for transfers between devices: 533 us -> none  [the longest x1 296 us: per_device(): lax.psum(jnp.stack(partials[15:19]).astype(jnp.bfloat16), 'tm')]
    ppermute x28 -> x0, starting transfers between devices: 109 us -> none  [passed_along(): return lax.ppermute(value, axis, pairs)]
    pallas_call x0 -> x3, Pallas kernels: none -> 80.8 us  [the longest x1 41.9 us: per_device(): pl.pallas_call(scatter_kernel, out_shape=tuple((shape(query.shape, BF16)...]
    dot_general x60 -> x0, matrix products: 42.2 us -> none  [the longest x10 13.9 us: attend(): jnp.einsum('hqk,khd->hqd', weights.astype(jnp.bfloat16), value_rows, pref...]
    ppermute x28 -> x0, waiting for transfers between devices: 34.8 us -> none  [passed_along(): return lax.ppermute(value, axis, pairs)]
    slice x22 -> x0, local copies, waits for them, and re-layouts: 22.5 us -> none  [the longest x16 16.7 us: attend(): member[1]]
    another operation x12 -> x0, other arithmetic: 12.7 us -> none
    and x3 -> x0, other arithmetic: 9.91 us -> none  [the longest x2 9.28 us: near_flag(): in_range & (key_frame <= query_frame) & (key_frame > query_frame - window)]
  transfers between devices with their start and end apart: 30 -> 0, of which waited for: 9 -> 0; matrix products, arithmetic and copies ran while one was open for 7% -> 0% of each run, Pallas kernels for 0% -> 0%
where the time goes in v1:
time: 90.9 us; the launch traced here: 89.8 us
  Pallas kernels  80.8 us (89%)
  local copies, waits for them, and re-layouts  7.72 us (8%)
  between operations  1.3 us (1%)
    pallas_call x1, Pallas kernels, per_device(): pl.pallas_call(scatter_kernel, out_shape=tuple((shape(query.shape, BF16)...  41.9 us
    pallas_call x1, Pallas kernels, per_device(): pl.pallas_call(gather_kernel, out_shape=(shape((rows, DH), BF16), shape((...  24.2 us
    pallas_call x1, Pallas kernels, per_device(): pl.pallas_call(attend_kernel, out_shape=(shape((rows, DH), BF16), shape((...  14.7 us
    unnamed x4, local copies, waits for them, and re-layouts  6.38 us

profile of v1, /device:TPU:102, one launch (start us, length us, event | category | flops | bytes accessed | tf_op | source)
XLA Modules:
  0.0 89.8 jit_solution(5279626307758641690)
XLA Ops:
  1.3 1.3 %broadcast_in_dim.2.w_ref = s32[5,8,128]{2,1,0:T(8,128)} broadcast(s32[5]{0:T(128)} %param.13), dimensions={0} | broadcast | bytes 20500 | tf_op jit(solution)/shard_map/broadcast_in_dim | solution.py:361
  2.6 24.2 %gather.1 = (bf16[1024,128]{1,0:T(8,128)(2,1)}, bf16[1024,128]{1,0:T(8,128)(2,1)}, bf16[32,2,128,128]{3,2,1,0:T(8,128)(2,1)}, s32[8,128]{1,0:T(8,128)}) custom-call(bf16[128,640]{1,0:T(8,128)(2,1)} %q_ref.1, bf16[128,640]{1,0:T(8,128)(2,1)} %k_ref.1, bf16[128,640]{1,0:T(8,128)(2,1)} %v_ref.1, bf16[128,640]{1,0:T(8,128)(2,1)} %do_ref.1, ...), custom_call_target="tpu_custom_call" | custom-call | tf_op jit(solution)/shard_map/gather/pallas_call | solution.py:362
  26.8 14.7 %attend.1 = (bf16[1024,128]{1,0:T(8,128)(2,1)}, bf16[1024,128]{1,0:T(8,128)(2,1)}, bf16[32,2,128,128]{3,2,1,0:T(8,128)(2,1)}) custom-call(s32[32]{0:T(128)} %fid_ref.1, s32[1]{0:T(128)S(6)} %copy.15.sink_ref, s32[8,128]{1,0:T(8,128)} %get-tuple-element.11.w_ref, bf16[1024,128]{1,0:T(8,128)(2,1)} %get-tuple-element.12.q_ref, ...), custom_call_target="tpu_custom_call" | custom-call | tf_op jit(solution)/shard_map/attend/pallas_call | solution.py:379
  41.5 41.9 %scatter.1 = (bf16[128,640]{1,0:T(8,128)(2,1)}, bf16[128,640]{1,0:T(8,128)(2,1)}, bf16[128,640]{1,0:T(8,128)(2,1)}, bf16[128,640]{1,0:T(8,128)(2,1)}) custom-call(bf16[1024,128]{1,0:T(8,128)(2,1)} %get-tuple-element.15.att_ref, bf16[1024,128]{1,0:T(8,128)(2,1)} %get-tuple-element.16.dq_ref, bf16[32,2,128,128]{3,2,1,0:T(8,128)(2,1)} %get-tuple-element.17.dkv_ref), custom_call_target="tpu_custom_call" | custom-call | tf_op jit(solution)/shard_map/scatter/pallas_call | solution.py:396
  83.4 1.6 %copy.16 = bf16[128,640]{1,0:T(8,128)(2,1)} copy(bf16[128,640]{1,0:T(8,128)(2,1)} %get-tuple-element.22) | data formatting | bytes 327680
  85.0 1.6 %copy.17 = bf16[128,640]{1,0:T(8,128)(2,1)} copy(bf16[128,640]{1,0:T(8,128)(2,1)} %get-tuple-element.23) | data formatting | bytes 327680
  86.6 1.6 %copy.18 = bf16[128,640]{1,0:T(8,128)(2,1)} copy(bf16[128,640]{1,0:T(8,128)(2,1)} %get-tuple-element.24) | data formatting | bytes 327680
  88.2 1.6 %copy.19 = bf16[128,640]{1,0:T(8,128)(2,1)} copy(bf16[128,640]{1,0:T(8,128)(2,1)} %get-tuple-element.25) | data formatting | bytes 327680

commit v2 on v1

v2 whole, which is shorter than its diff:
```python
import math

import jax
import jax.numpy as jnp
from jax import lax
from jax.experimental import pallas as pl
from jax.experimental.pallas import tpu as pltpu
from jax.sharding import PartitionSpec as P

MESH = pl.DeviceIdType.MESH
BLK = 128
DH = 128
HPD = 5
RING = 4
PLANE = 8
AHEAD = 3
NBLK = RING * PLANE
BF16 = jnp.bfloat16
F32 = jnp.float32
TILE_Q = 2 * BLK
MAX_CHUNKS = 5
NEG = -1e30


def seat_of(u):
    if u < 8:
        return 2 * (u % 4) + u // 4, (u % 4 + u // 4) % 2
    return ((0, 1), (5, 0))[u - 8]


def position():
    tm = lax.axis_index("tm")
    head = lax.axis_index("head")
    return tm // PLANE, tm % PLANE, head // 2, head % 2


def owner_ids(y):
    _, _, x_lo, core = position()
    half = y // 2
    ids = []
    for j in range(HPD):
        (p0, e0), (p1, e1) = seat_of(j), seat_of(HPD + j)
        place = p0 + core * (p1 - p0)
        e = e0 + core * (e1 - e0)
        row = (1 - half) * (1 - e) + half * (2 + e)
        ids.append((row * PLANE + place, 2 * (1 - x_lo) + y % 2))
    return ids


def my_task():
    row, place, x_lo, core = position()
    half = row // 2
    e = half * (row - 2) + (1 - half) * (1 - row)
    other = (e + place // 2 + place % 2) % 2
    u = (1 - other) * (4 * (place % 2) + place // 2) + other * (8 + place // 5)
    is_owner = (other == 0) | (place == 0) | (place == 5)
    return is_owner, 2 * half + core, 2 * (1 - x_lo) + u // HPD, u % HPD


def neighbours():
    row, place, x_lo, core = position()
    tm = row * PLANE + place
    across = (RING - 1 - row) * PLANE + place
    same, swapped = 2 * x_lo + core, 2 * x_lo + 1 - core
    return (tm, swapped), (across, same), (across, swapped)


def signal(device):
    pl.semaphore_signal(
        pltpu.get_barrier_semaphore(), inc=1, device_id=device, device_id_type=MESH
    )


def wait_for(count):
    pl.semaphore_wait(pltpu.get_barrier_semaphore(), count)


def send(src, dst, send_sem, recv_sem, device):
    pltpu.make_async_remote_copy(
        src_ref=src, dst_ref=dst, send_sem=send_sem, recv_sem=recv_sem,
        device_id=device, device_id_type=MESH,
    ).start()


def settle(ref, sem):
    pltpu.make_async_copy(ref, ref, sem).wait()


def gather_kernel(
    q_ref, k_ref, v_ref, do_ref, w_ref,
    qo_ref, doo_ref, kvo_ref, wo_ref,
    send_sem, ahead_send, w_send, qd_sem, kv_sem, w_sem, ahead_sem,
    sib_sem, cross_sem, relay_sem, sib_send, cross_send, relay_send,
):
    y, place, _, _ = position()
    is_owner, plane, src_head, _ = my_task()
    sibling, across, _ = neighbours()
    even = plane % 2 == 0
    early = plane < 2
    looked_at = (y == 2) & (place < AHEAD)

    @pl.when(is_owner)
    def _():
        for r in range(PLANE):
            signal((plane * PLANE + r, src_head))
        signal(sibling)
        pl.when(jnp.logical_not(early))(lambda: signal(across))

        @pl.when(plane == 1)
        def _():
            for r in range(AHEAD):
                signal((2 * PLANE + r, src_head))

    wait_for(
        jnp.where(looked_at, 2 * HPD, HPD)
        + jnp.where(is_owner, 1, 0)
        + jnp.where(is_owner & early, 1, 0)
    )

    def column(ref, j):
        return ref.at[:, pl.ds(j * DH, DH)]

    rows = pl.ds(pl.multiple_of(place * BLK, BLK), BLK)
    targets = owner_ids(y)
    tile = y * PLANE + place
    for j in range(HPD):
        for part, ref in enumerate((k_ref, v_ref)):
            send(column(ref, j), kvo_ref.at[tile, part], send_sem.at[part], kv_sem.at[place],
                 targets[j])

    @pl.when(looked_at)
    def _():
        for j, device in enumerate(owner_ids(1)):
            for part, ref in enumerate((k_ref, v_ref)):
                send(column(ref, j), kvo_ref.at[tile, part], ahead_send.at[part],
                     ahead_sem.at[place], device)

    for j in range(HPD):
        for part, (ref, out) in enumerate(((q_ref, qo_ref), (do_ref, doo_ref))):
            send(column(ref, j), out.at[rows], send_sem.at[2 + part], qd_sem.at[part], targets[j])

    @pl.when(place == 0)
    def _():
        for j in range(HPD):
            send(w_ref, wo_ref, w_send.at[j], w_sem, targets[j])

    @pl.when(is_owner)
    def _():
        base = plane * PLANE

        def pass_on(block, to, recv, sent):
            send(kvo_ref.at[block], kvo_ref.at[block], sent, recv, to)

        for r in range(PLANE):
            settle(kvo_ref.at[base + r], kv_sem.at[r])
            pl.when(early)(lambda r=r: pass_on(base + r, across, cross_sem.at[r], cross_send))
            if r < AHEAD:
                pass_on(base + r, sibling, sib_sem.at[r], sib_send)
            else:
                pl.when(even)(lambda r=r: pass_on(base + r, sibling, sib_sem.at[r], sib_send))

        @pl.when(jnp.logical_not(early))
        def _():
            mine = (plane - 2) * PLANE
            theirs = (1 - (plane - 2)) * PLANE
            for r in range(PLANE):
                settle(kvo_ref.at[mine + r], cross_sem.at[r])
                pass_on(mine + r, sibling, relay_sem.at[r], relay_send)
            for r in range(PLANE):
                settle(kvo_ref.at[theirs + r], relay_sem.at[r])
            settle(kvo_ref.at[pl.ds(0, PLANE)], relay_send)

        beside = (plane + 1 - 2 * (plane % 2)) * PLANE
        for r in range(AHEAD):
            settle(kvo_ref.at[beside + r], sib_sem.at[r])

        @pl.when(jnp.logical_not(even))
        def _():
            for r in range(AHEAD, PLANE):
                settle(kvo_ref.at[beside + r], sib_sem.at[r])

        @pl.when(plane == 1)
        def _():
            for r in range(AHEAD):
                settle(kvo_ref.at[2 * PLANE + r], ahead_sem.at[r])

        settle(qo_ref, qd_sem.at[0])
        settle(doo_ref, qd_sem.at[1])
        settle(wo_ref, w_sem)
        pl.when(early)(lambda: settle(kvo_ref.at[pl.ds(0, PLANE)], cross_send))
        pl.when(even)(lambda: settle(kvo_ref.at[pl.ds(0, PLANE)], sib_send))
        pl.when(jnp.logical_not(even))(
            lambda: settle(kvo_ref.at[pl.ds(0, AHEAD)], sib_send)
        )

    for part, ref in enumerate((k_ref, v_ref, q_ref, do_ref)):
        settle(ref, send_sem.at[part])

    @pl.when(looked_at)
    def _():
        settle(k_ref, ahead_send.at[0])
        settle(v_ref, ahead_send.at[1])

    @pl.when(place == 0)
    def _():
        for j in range(HPD):
            settle(w_ref, w_send.at[j])


def attend_kernel(
    fid_ref, sink_ref, w_ref, q_ref, do_ref, kv_ref,
    att_ref, dq_ref, dkv_ref,
    t_s, p_s, dk_s, dv_s,
):
    is_owner, y, _, src_j = my_task()
    scale = 1.0 / math.sqrt(DH)
    slope = scale * math.log2(math.e)
    chunk = 4 * BLK

    @pl.when(is_owner)
    def _():
        c = 1 + fid_ref[1] + fid_ref[2]
        sink = sink_ref[0]
        win = w_ref[src_j]
        dk_s[...] = jnp.zeros_like(dk_s)
        dv_s[...] = jnp.zeros_like(dv_s)
        lane = lax.broadcasted_iota(jnp.int32, (1, TILE_Q), 1)

        def sees(query_frame, frame):
            near = (frame <= query_frame) & (frame > query_frame - win)
            return near | ((frame == sink) & (sink <= query_frame))

        @pl.loop(0, PLANE // 2)
        def _(t):
            rows = pl.ds(pl.multiple_of(t * TILE_Q, TILE_Q), TILE_Q)
            block_a = y * PLANE + 2 * t
            frame_a = (block_a + c) // 4
            frame_b = (block_a + 1 + c) // 4
            low = jnp.maximum(frame_a - win + 1, 0)
            near_count = frame_b - low + 1
            count = near_count + (sink < low).astype(jnp.int32)

            def frame_at(i):
                return jnp.where(i < near_count, low + i, sink)

            def start_of(frame):
                return jnp.clip(4 * frame - c, 0, NBLK - 4)

            q_tile = q_ref[rows]
            q_t = q_tile.T

            def scores(i, top):
                frame = frame_at(i)
                start = start_of(frame)
                see_a = sees(frame_a, frame)
                see_b = sees(frame_b, frame)
                keys = kv_ref[pl.ds(start, 4), 0].reshape(chunk, DH)
                s = jnp.dot(keys, q_t, preferred_element_type=F32)
                for k in range(4):
                    here = (start + k + c) // 4 == frame
                    bias = jnp.where(
                        lane < BLK,
                        jnp.where(here & see_a, 0.0, NEG),
                        jnp.where(here & see_b, 0.0, NEG),
                    )
                    part = s[k * BLK : (k + 1) * BLK] + bias
                    t_s[pl.ds(i * chunk + k * BLK, BLK), :] = part
                    top = jnp.maximum(top, jnp.max(part.reshape(BLK // 8, 8, TILE_Q), axis=0))
                return top

            top = lax.fori_loop(0, count, scores, jnp.full((8, TILE_Q), NEG, F32))
            top = jnp.max(top, axis=0, keepdims=True) * slope

            def mix(i, carry):
                total, mixed = carry
                start = start_of(frame_at(i))
                at = pl.ds(pl.multiple_of(i * chunk, chunk), chunk)
                p = jnp.exp2(t_s[at, :] * slope - top)
                total = total + jnp.sum(p.reshape(chunk // 8, 8, TILE_Q), axis=0)
                p = p.astype(BF16)
                p_s[at, :] = p
                values = kv_ref[pl.ds(start, 4), 1].reshape(chunk, DH)
                mixed = mixed + lax.dot_general(
                    values, p, (((0,), (0,)), ((), ())), preferred_element_type=F32
                )
                return total, mixed

            total, mixed = lax.fori_loop(
                0, count, mix, (jnp.zeros((8, TILE_Q), F32), jnp.zeros((DH, TILE_Q), F32))
            )
            inverse = 1.0 / jnp.sum(total, axis=0, keepdims=True)
            att_t = (mixed * inverse).astype(BF16)
            att_ref[rows] = att_t.T
            do_t = (do_ref[rows].T.astype(F32) * inverse).astype(BF16)
            do_n = do_t.T
            delta = jnp.sum(do_t.astype(F32) * att_t.astype(F32), axis=0, keepdims=True)

            def back(i, dq_t):
                start = start_of(frame_at(i))
                at = pl.ds(pl.multiple_of(i * chunk, chunk), chunk)
                keys = kv_ref[pl.ds(start, 4), 0].reshape(chunk, DH)
                values = kv_ref[pl.ds(start, 4), 1].reshape(chunk, DH)
                p = p_s[at, :]
                dp = jnp.dot(values, do_t, preferred_element_type=F32)
                g = (p.astype(F32) * (dp - delta)).astype(BF16)
                dk = jnp.dot(g, q_tile, preferred_element_type=F32)
                dv = jnp.dot(p, do_n, preferred_element_type=F32)
                dk_s[pl.ds(start, 4)] += dk.reshape(4, BLK, DH)
                dv_s[pl.ds(start, 4)] += dv.reshape(4, BLK, DH)
                return dq_t + lax.dot_general(
                    keys, g, (((0,), (0,)), ((), ())), preferred_element_type=F32
                )

            dq_t = lax.fori_loop(0, count, back, jnp.zeros((DH, TILE_Q), F32))
            dq_ref[rows] = (dq_t * scale).astype(BF16).T

        @pl.loop(0, NBLK)
        def _(b):
            dkv_ref[b, 0] = (dk_s[b] * scale).astype(BF16)
            dkv_ref[b, 1] = dv_s[b].astype(BF16)


def scatter_kernel(
    att_ref, dq_ref, dkv_ref,
    atto_ref, dqo_ref, dko_ref, dvo_ref,
    keep, beside, over, back, ahead, far, joined, done, acc,
    keep_sem, far_sem, out_send, out_sem, done_send,
    beside_send, beside_sem, over_send, over_sem, joined_send, back_sem, ahead_send, ahead_sem,
):
    y, place, _, _ = position()
    is_owner, plane, src_head, j_there = my_task()
    sibling, across, diagonal = neighbours()
    even = plane % 2 == 0
    early = plane < 2
    late = jnp.logical_not(early)
    base = plane * PLANE
    column = pl.ds(pl.multiple_of(j_there * DH, DH), DH)

    for device in owner_ids(y):
        signal(device)

    @pl.when(is_owner)
    def _():
        signal(sibling)
        pl.when(early)(lambda: signal(across))
        pl.when(plane == 2)(lambda: signal(diagonal))
        mine = pltpu.make_async_copy(dkv_ref.at[pl.ds(base, PLANE)], keep, keep_sem)
        mine.start()
        low = (plane % 2) * PLANE
        other_low = (1 - plane % 2) * PLANE
        theirs = pltpu.make_async_copy(dkv_ref.at[pl.ds(low, PLANE)], far, far_sem)
        pl.when(late)(theirs.start)
        wait_for(jnp.where(late | (plane == 1), PLANE + 2, PLANE + 1))

        next_to = (plane + 1 - 2 * (plane % 2)) * PLANE

        @pl.when(late)
        def _():
            for r in range(PLANE):
                send(dkv_ref.at[other_low + r], over.at[r], over_send, over_sem.at[r], sibling)

        for r in range(PLANE):
            def to_sibling(r=r):
                send(dkv_ref.at[next_to + r], beside.at[r], beside_send, beside_sem.at[r], sibling)

            if r < AHEAD:
                to_sibling()
            else:
                pl.when(jnp.logical_not(even))(to_sibling)

        @pl.when(plane == 1)
        def _():
            for r in range(AHEAD):
                send(dkv_ref.at[2 * PLANE + r], ahead.at[r], ahead_send, ahead_sem.at[r], diagonal)

        @pl.when(late)
        def _():
            theirs.wait()
            for r in range(PLANE):
                settle(over.at[r], over_sem.at[r])
                joined[r] = (over[r].astype(F32) + far[r].astype(F32)).astype(BF16)
                send(joined.at[r], back.at[r], joined_send, back_sem.at[r], across)

        for r in range(PLANE):
            for part, (ref, out) in enumerate(((att_ref, atto_ref), (dq_ref, dqo_ref))):
                send(ref.at[pl.ds(r * BLK, BLK)], out.at[:, column], out_send.at[part],
                     out_sem.at[part], (base + r, src_head))
        mine.wait()
        for r in range(PLANE):
            acc[...] = keep[r].astype(F32)

            def add(buffer, sems, r=r):
                settle(buffer.at[r], sems.at[r])
                acc[...] += buffer[r].astype(F32)

            if r < AHEAD:
                add(beside, beside_sem)
                pl.when(plane == 2)(lambda add=add: add(ahead, ahead_sem))
            else:
                pl.when(even)(lambda add=add: add(beside, beside_sem))
            pl.when(early)(lambda add=add: add(back, back_sem))
            done[r] = acc[...].astype(BF16)
            for part, out in enumerate((dko_ref, dvo_ref)):
                send(done.at[r, part], out.at[:, column], done_send, out_sem.at[2 + part],
                     (base + r, src_head))
        settle(att_ref, out_send.at[0])
        settle(dq_ref, out_send.at[1])
        settle(done, done_send)
        pl.when(even)(lambda: settle(ahead, beside_send))
        pl.when(jnp.logical_not(even))(lambda: settle(done, beside_send))
        pl.when(plane == 1)(lambda: settle(ahead, ahead_send))

        @pl.when(late)
        def _():
            settle(done, over_send)
            settle(joined, joined_send)

    for part, ref in enumerate((atto_ref, dqo_ref, dko_ref, dvo_ref)):
        settle(ref, out_sem.at[part])


def finish_kernel(*refs):
    for src, out in zip(refs[:4], refs[4:]):
        out[...] = src[...]


def per_device(query, key, value, grad_out, frame_ids, sink_frame, window):
    any_spec = pl.BlockSpec(memory_space=pl.ANY)
    smem = pl.BlockSpec(memory_space=pltpu.SMEM)
    vmem = pl.BlockSpec(memory_space=pltpu.VMEM)
    dma = pltpu.SemaphoreType.DMA
    shape = jax.ShapeDtypeStruct
    rows = PLANE * BLK
    q_all, do_all, kv_all, w_all = pl.pallas_call(
        gather_kernel,
        out_shape=(
            shape((rows, DH), BF16),
            shape((rows, DH), BF16),
            shape((NBLK, 2, BLK, DH), BF16),
            shape((HPD,), jnp.int32),
        ),
        in_specs=[any_spec] * 5,
        out_specs=[any_spec] * 4,
        scratch_shapes=[
            dma((4,)), dma((2,)), dma((HPD,)), dma((2,)), dma((PLANE,)), dma, dma((AHEAD,)),
            dma((PLANE,)), dma((PLANE,)), dma((PLANE,)), dma, dma, dma,
        ],
        compiler_params=pltpu.CompilerParams(collective_id=0, has_side_effects=True),
        name="gather",
    )(query, key, value, grad_out, window)
    att, dq, dkv = pl.pallas_call(
        attend_kernel,
        out_shape=(
            shape((rows, DH), BF16),
            shape((rows, DH), BF16),
            shape((NBLK, 2, BLK, DH), BF16),
        ),
        in_specs=[smem] * 3 + [vmem] * 3,
        out_specs=[vmem] * 3,
        scratch_shapes=[
            pltpu.VMEM((MAX_CHUNKS * 4 * BLK, TILE_Q), F32),
            pltpu.VMEM((MAX_CHUNKS * 4 * BLK, TILE_Q), BF16),
            pltpu.VMEM((NBLK, BLK, DH), F32),
            pltpu.VMEM((NBLK, BLK, DH), F32),
        ],
        name="attend",
    )(frame_ids, sink_frame, w_all, q_all, do_all, kv_all)

    def tiles(count):
        return pltpu.VMEM((count, 2, BLK, DH), BF16)

    outs = pl.pallas_call(
        scatter_kernel,
        out_shape=tuple(shape(query.shape, BF16) for _ in range(4)),
        in_specs=[any_spec] * 3,
        out_specs=[any_spec] * 4,
        scratch_shapes=[
            tiles(PLANE), tiles(PLANE), tiles(PLANE), tiles(PLANE), tiles(AHEAD), tiles(PLANE),
            tiles(PLANE), tiles(PLANE), pltpu.VMEM((2, BLK, DH), F32),
            dma, dma, dma((2,)), dma((4,)), dma,
            dma, dma((PLANE,)), dma, dma((PLANE,)), dma, dma((PLANE,)), dma, dma((AHEAD,)),
        ],
        compiler_params=pltpu.CompilerParams(collective_id=1, has_side_effects=True),
        name="scatter",
    )(att, dq, dkv)
    return pl.pallas_call(
        finish_kernel,
        out_shape=tuple(shape(query.shape, BF16) for _ in range(4)),
        in_specs=[vmem] * 4,
        out_specs=[vmem] * 4,
        name="finish",
    )(*outs)


def solution(mesh):
    tm_head = P("tm", "head")
    return jax.shard_map(
        per_device,
        mesh=mesh,
        in_specs=(tm_head, tm_head, tm_head, tm_head, P(), P(), P("head")),
        out_specs=(tm_head, tm_head, tm_head, tm_head),
        check_vma=False,
    )
```

time: 90.9 us -> 73.9 us (0.81)
  Pallas kernels: 80.8 us -> 72.4 us
  local copies, waits for them, and re-layouts: 7.72 us -> 0 us
    pallas_call x1, Pallas kernels: 41.9 us -> 56.7 us  [per_device(): pl.pallas_call(scatter_kernel, out_shape=tuple((shape(query.shape, BF16)...]
    pallas_call x1, Pallas kernels: 24.2 us -> 10.3 us  [per_device(): pl.pallas_call(gather_kernel, out_shape=(shape((rows, DH), BF16), shape((...]
    pallas_call x1, Pallas kernels: 14.7 us -> 3.33 us  [per_device(): pl.pallas_call(attend_kernel, out_shape=(shape((rows, DH), BF16), shape((...]
    unnamed x4 -> x0, local copies, waits for them, and re-layouts: 6.38 us -> none
    pallas_call x0 -> x1, Pallas kernels: none -> 2 us  [per_device(): pl.pallas_call(finish_kernel, out_shape=tuple((shape(query.shape, BF16) f...]
    broadcast_in_dim x1 -> x0, local copies, waits for them, and re-layouts: 1.33 us -> none  [per_device(): windows = jnp.broadcast_to(window[:, None, None], (HPD, 8, 128))]
where the time goes in v2:
time: 73.9 us; the launch traced here: 73.7 us
  Pallas kernels  72.4 us (98%)
  between operations  1.3 us (2%)
    pallas_call x1, Pallas kernels, per_device(): pl.pallas_call(scatter_kernel, out_shape=tuple((shape(query.shape, BF16)...  56.7 us
    pallas_call x1, Pallas kernels, per_device(): pl.pallas_call(gather_kernel, out_shape=(shape((rows, DH), BF16), shape((...  10.3 us
    pallas_call x1, Pallas kernels, per_device(): pl.pallas_call(attend_kernel, out_shape=(shape((rows, DH), BF16), shape((...  3.33 us
    pallas_call x1, Pallas kernels, per_device(): pl.pallas_call(finish_kernel, out_shape=tuple((shape(query.shape, BF16) f...  2 us

profile of v2, /device:TPU:102, one launch (start us, length us, event | category | flops | bytes accessed | tf_op | source)
XLA Modules:
  0.0 73.7 jit_solution(9071280400333386716)
XLA Ops:
  1.3 10.3 %gather.1 = (bf16[1024,128]{1,0:T(8,128)(2,1)}, bf16[1024,128]{1,0:T(8,128)(2,1)}, bf16[32,2,128,128]{3,2,1,0:T(8,128)(2,1)}, s32[5]{0:T(128)}) custom-call(bf16[128,640]{1,0:T(8,128)(2,1)} %q_ref.1, bf16[128,640]{1,0:T(8,128)(2,1)} %k_ref.1, bf16[128,640]{1,0:T(8,128)(2,1)} %v_ref.1, bf16[128,640]{1,0:T(8,128)(2,1)} %do_ref.1, s32[5]{0:T(128)} %w_ref.1), custom_call_target="tpu_custom_call" | custom-call | tf_op jit(solution)/shard_map/gather/pallas_call | solution.py:434
  11.6 3.3 %attend.1 = (bf16[1024,128]{1,0:T(8,128)(2,1)}, bf16[1024,128]{1,0:T(8,128)(2,1)}, bf16[32,2,128,128]{3,2,1,0:T(8,128)(2,1)}) custom-call(s32[32]{0:T(128)} %fid_ref.1, s32[1]{0:T(128)S(6)} %copy.11.sink_ref, s32[5]{0:T(128)} %get-tuple-element.15.w_ref, bf16[1024,128]{1,0:T(8,128)(2,1)} %get-tuple-element.16.q_ref, ...), custom_call_target="tpu_custom_call" | custom-call | tf_op jit(solution)/shard_map/attend/pallas_call | solution.py:451
  15.0 56.7 %scatter.1 = (bf16[128,640]{1,0:T(8,128)(2,1)}, bf16[128,640]{1,0:T(8,128)(2,1)}, bf16[128,640]{1,0:T(8,128)(2,1)}, bf16[128,640]{1,0:T(8,128)(2,1)}) custom-call(bf16[1024,128]{1,0:T(8,128)(2,1)} %get-tuple-element.19.att_ref, bf16[1024,128]{1,0:T(8,128)(2,1)} %get-tuple-element.20.dq_ref, bf16[32,2,128,128]{3,2,1,0:T(8,128)(2,1)} %get-tuple-element.21.dkv_ref), custom_call_target="tpu_custom_call" | custom-call | tf_op jit(solution)/shard_map/scatter/pallas_call | solution.py:472
  71.7 2.0 %finish.1 = (bf16[128,640]{1,0:T(8,128)(2,1)}, bf16[128,640]{1,0:T(8,128)(2,1)}, bf16[128,640]{1,0:T(8,128)(2,1)}, bf16[128,640]{1,0:T(8,128)(2,1)}) custom-call(bf16[128,640]{1,0:T(8,128)(2,1)} %get-tuple-element.22.refs_0_, bf16[128,640]{1,0:T(8,128)(2,1)} %get-tuple-element.23.refs_1_, bf16[128,640]{1,0:T(8,128)(2,1)} %get-tuple-element.24.refs_2_, ...), custom_call_target="tpu_custom_call" | custom-call | tf_op jit(solution)/shard_map/finish/pallas_call | solution.py:486

commit v3 on v2

--- a/solution.py
+++ b/solution.py
@@ -20,6 +20,7 @@
 TILE_Q = 2 * BLK
 MAX_CHUNKS = 5
 NEG = -1e30
+MIB = 1 << 20
 
 
 def seat_of(u):
@@ -373,6 +374,11 @@
             for r in range(AHEAD):
                 send(dkv_ref.at[2 * PLANE + r], ahead.at[r], ahead_send, ahead_sem.at[r], diagonal)
 
+        for r in range(PLANE):
+            for part, (ref, out) in enumerate(((att_ref, atto_ref), (dq_ref, dqo_ref))):
+                send(ref.at[pl.ds(r * BLK, BLK)], out.at[:, column], out_send.at[part],
+                     out_sem.at[part], (base + r, src_head))
+
         @pl.when(late)
         def _():
             theirs.wait()
@@ -381,10 +387,6 @@
                 joined[r] = (over[r].astype(F32) + far[r].astype(F32)).astype(BF16)
                 send(joined.at[r], back.at[r], joined_send, back_sem.at[r], across)
 
-        for r in range(PLANE):
-            for part, (ref, out) in enumerate(((att_ref, atto_ref), (dq_ref, dqo_ref))):
-                send(ref.at[pl.ds(r * BLK, BLK)], out.at[:, column], out_send.at[part],
-                     out_sem.at[part], (base + r, src_head))
         mine.wait()
         for r in range(PLANE):
             acc[...] = keep[r].astype(F32)
@@ -424,6 +426,14 @@
         out[...] = src[...]
 
 
+def in_vmem(array):
+    return pltpu.with_memory_space_constraint(array, pltpu.VMEM)
+
+
+def in_hbm(array):
+    return pltpu.with_memory_space_constraint(array, pltpu.HBM)
+
+
 def per_device(query, key, value, grad_out, frame_ids, sink_frame, window):
     any_spec = pl.BlockSpec(memory_space=pl.ANY)
     smem = pl.BlockSpec(memory_space=pltpu.SMEM)
@@ -434,9 +444,9 @@
     q_all, do_all, kv_all, w_all = pl.pallas_call(
         gather_kernel,
         out_shape=(
-            shape((rows, DH), BF16),
-            shape((rows, DH), BF16),
-            shape((NBLK, 2, BLK, DH), BF16),
+            pltpu.VMEM((rows, DH), BF16),
+            pltpu.VMEM((rows, DH), BF16),
+            pltpu.VMEM((NBLK, 2, BLK, DH), BF16),
             shape((HPD,), jnp.int32),
         ),
         in_specs=[any_spec] * 5,
@@ -445,15 +455,17 @@
             dma((4,)), dma((2,)), dma((HPD,)), dma((2,)), dma((PLANE,)), dma, dma((AHEAD,)),
             dma((PLANE,)), dma((PLANE,)), dma((PLANE,)), dma, dma, dma,
         ],
-        compiler_params=pltpu.CompilerParams(collective_id=0, has_side_effects=True),
+        compiler_params=pltpu.CompilerParams(
+            collective_id=0, has_side_effects=True, vmem_limit_bytes=8 * MIB
+        ),
         name="gather",
-    )(query, key, value, grad_out, window)
+    )(*[in_hbm(array) for array in (query, key, value, grad_out, window)])
     att, dq, dkv = pl.pallas_call(
         attend_kernel,
         out_shape=(
-            shape((rows, DH), BF16),
-            shape((rows, DH), BF16),
-            shape((NBLK, 2, BLK, DH), BF16),
+            pltpu.VMEM((rows, DH), BF16),
+            pltpu.VMEM((rows, DH), BF16),
+            pltpu.VMEM((NBLK, 2, BLK, DH), BF16),
         ),
         in_specs=[smem] * 3 + [vmem] * 3,
         out_specs=[vmem] * 3,
@@ -463,15 +475,16 @@
             pltpu.VMEM((NBLK, BLK, DH), F32),
             pltpu.VMEM((NBLK, BLK, DH), F32),
         ],
+        compiler_params=pltpu.CompilerParams(vmem_limit_bytes=32 * MIB),
         name="attend",
-    )(frame_ids, sink_frame, w_all, q_all, do_all, kv_all)
+    )(in_hbm(frame_ids), sink_frame, w_all, in_vmem(q_all), in_vmem(do_all), in_vmem(kv_all))
 
     def tiles(count):
         return pltpu.VMEM((count, 2, BLK, DH), BF16)
 
     outs = pl.pallas_call(
         scatter_kernel,
-        out_shape=tuple(shape(query.shape, BF16) for _ in range(4)),
+        out_shape=tuple(pltpu.VMEM(query.shape, BF16) for _ in range(4)),
         in_specs=[any_spec] * 3,
         out_specs=[any_spec] * 4,
         scratch_shapes=[
@@ -480,16 +493,19 @@
             dma, dma, dma((2,)), dma((4,)), dma,
             dma, dma((PLANE,)), dma, dma((PLANE,)), dma, dma((PLANE,)), dma, dma((AHEAD,)),
         ],
-        compiler_params=pltpu.CompilerParams(collective_id=1, has_side_effects=True),
+        compiler_params=pltpu.CompilerParams(
+            collective_id=1, has_side_effects=True, vmem_limit_bytes=16 * MIB
+        ),
         name="scatter",
-    )(att, dq, dkv)
+    )(in_vmem(att), in_vmem(dq), in_vmem(dkv))
     return pl.pallas_call(
         finish_kernel,
         out_shape=tuple(shape(query.shape, BF16) for _ in range(4)),
         in_specs=[vmem] * 4,
         out_specs=[vmem] * 4,
+        compiler_params=pltpu.CompilerParams(vmem_limit_bytes=8 * MIB),
         name="finish",
-    )(*outs)
+    )(*[in_vmem(out) for out in outs])
 
 
 def solution(mesh):

time: 73.9 us -> 67.6 us (0.915)
  Pallas kernels: 72.4 us -> 66.1 us
    pallas_call x3, Pallas kernels: 70.4 us -> 65.3 us  [the longest x1 54.2 us: per_device(): pl.pallas_call(scatter_kernel, out_shape=tuple((pltpu.VMEM(query.shape, B...]
    pallas_call x1, Pallas kernels: 2 us -> 0.88 us  [per_device(): pl.pallas_call(finish_kernel, out_shape=tuple((shape(query.shape, BF16) f...]
where the time goes in v3:
time: 67.6 us; the launch traced here: 67.4 us
  Pallas kernels  66.1 us (98%)
  between operations  1.3 us (2%)
    pallas_call x1, Pallas kernels, per_device(): pl.pallas_call(scatter_kernel, out_shape=tuple((pltpu.VMEM(query.shape, B...  54.2 us
    pallas_call x1, Pallas kernels, per_device(): pl.pallas_call(gather_kernel, out_shape=(pltpu.VMEM((rows, DH), BF16), pl...  10.3 us

profile of v3, /device:TPU:102, one launch (start us, length us, event | category | flops | bytes accessed | tf_op | source)
XLA Modules:
  0.0 67.4 jit_solution(7117963553052061697)
XLA Ops:
  1.3 10.3 %gather.1 = (bf16[1024,128]{1,0:T(8,128)(2,1)S(1)}, bf16[1024,128]{1,0:T(8,128)(2,1)S(1)}, bf16[32,2,128,128]{3,2,1,0:T(8,128)(2,1)S(1)}, s32[5]{0:T(128)S(1)}) custom-call(bf16[128,640]{1,0:T(8,128)(2,1)} %q_ref.1, bf16[128,640]{1,0:T(8,128)(2,1)} %k_ref.1, bf16[128,640]{1,0:T(8,128)(2,1)} %v_ref.1, bf16[128,640]{1,0:T(8,128)(2,1)} %do_ref.1, s32[5]{0:T(128)} %w_ref.1), custom_call_target="tpu_custom_call" | custom-call | tf_op jit(solution)/shard_map/gather/pallas_call | solution.py:444
  11.6 0.7 %attend.1 = (bf16[1024,128]{1,0:T(8,128)(2,1)S(1)}, bf16[1024,128]{1,0:T(8,128)(2,1)S(1)}, bf16[32,2,128,128]{3,2,1,0:T(8,128)(2,1)S(1)}) custom-call(s32[32]{0:T(128)} %fid_ref.1, s32[1]{0:T(128)S(6)} %copy.11.sink_ref, s32[5]{0:T(128)S(1)} %get-tuple-element.15.w_ref, bf16[1024,128]{1,0:T(8,128)(2,1)S(1)} %get-tuple-element.16.q_ref, ...), custom_call_target="tpu_custom_call" | custom-call | tf_op jit(solution)/shard_map/attend/pallas_call | solution.py:463
  12.4 54.2 %scatter.1 = (bf16[128,640]{1,0:T(8,128)(2,1)S(1)}, bf16[128,640]{1,0:T(8,128)(2,1)S(1)}, bf16[128,640]{1,0:T(8,128)(2,1)S(1)}, bf16[128,640]{1,0:T(8,128)(2,1)S(1)}) custom-call(bf16[1024,128]{1,0:T(8,128)(2,1)S(1)} %get-tuple-element.19.att_ref, bf16[1024,128]{1,0:T(8,128)(2,1)S(1)} %get-tuple-element.20.dq_ref, ...), custom_call_target="tpu_custom_call" | custom-call | tf_op jit(solution)/shard_map/scatter/pallas_call | solution.py:485
  66.6 0.9 %finish.1 = (bf16[128,640]{1,0:T(8,128)(2,1)}, bf16[128,640]{1,0:T(8,128)(2,1)}, bf16[128,640]{1,0:T(8,128)(2,1)}, bf16[128,640]{1,0:T(8,128)(2,1)}) custom-call(bf16[128,640]{1,0:T(8,128)(2,1)S(1)} %get-tuple-element.22.refs_0_, bf16[128,640]{1,0:T(8,128)(2,1)S(1)} %get-tuple-element.23.refs_1_, bf16[128,640]{1,0:T(8,128)(2,1)S(1)} %get-tuple-element.24.refs_2_, ...), custom_call_target="tpu_custom_call" | custom-call | tf_op jit(solution)/shard_map/finish/pallas_call | solution.py:501

commit v4 on v3

--- a/solution.py
+++ b/solution.py
@@ -324,8 +324,8 @@
 def scatter_kernel(
     att_ref, dq_ref, dkv_ref,
     atto_ref, dqo_ref, dko_ref, dvo_ref,
-    keep, beside, over, back, ahead, far, joined, done, acc,
-    keep_sem, far_sem, out_send, out_sem, done_send,
+    beside, over, back, ahead, joined, done, acc,
+    out_send, out_sem, done_send,
     beside_send, beside_sem, over_send, over_sem, joined_send, back_sem, ahead_send, ahead_sem,
 ):
     y, place, _, _ = position()
@@ -345,12 +345,8 @@
         signal(sibling)
         pl.when(early)(lambda: signal(across))
         pl.when(plane == 2)(lambda: signal(diagonal))
-        mine = pltpu.make_async_copy(dkv_ref.at[pl.ds(base, PLANE)], keep, keep_sem)
-        mine.start()
         low = (plane % 2) * PLANE
         other_low = (1 - plane % 2) * PLANE
-        theirs = pltpu.make_async_copy(dkv_ref.at[pl.ds(low, PLANE)], far, far_sem)
-        pl.when(late)(theirs.start)
         wait_for(jnp.where(late | (plane == 1), PLANE + 2, PLANE + 1))
 
         next_to = (plane + 1 - 2 * (plane % 2)) * PLANE
@@ -359,6 +355,13 @@
         def _():
             for r in range(PLANE):
                 send(dkv_ref.at[other_low + r], over.at[r], over_send, over_sem.at[r], sibling)
+
+        @pl.when(late)
+        def _():
+            for r in range(PLANE):
+                settle(over.at[r], over_sem.at[r])
+                joined[r] = (over[r].astype(F32) + dkv_ref[low + r].astype(F32)).astype(BF16)
+                send(joined.at[r], back.at[r], joined_send, back_sem.at[r], across)
 
         for r in range(PLANE):
             def to_sibling(r=r):
@@ -379,17 +382,8 @@
                 send(ref.at[pl.ds(r * BLK, BLK)], out.at[:, column], out_send.at[part],
                      out_sem.at[part], (base + r, src_head))
 
-        @pl.when(late)
-        def _():
-            theirs.wait()
-            for r in range(PLANE):
-                settle(over.at[r], over_sem.at[r])
-                joined[r] = (over[r].astype(F32) + far[r].astype(F32)).astype(BF16)
-                send(joined.at[r], back.at[r], joined_send, back_sem.at[r], across)
-
-        mine.wait()
         for r in range(PLANE):
-            acc[...] = keep[r].astype(F32)
+            acc[...] = dkv_ref[base + r].astype(F32)
 
             def add(buffer, sems, r=r):
                 settle(buffer.at[r], sems.at[r])
@@ -485,12 +479,12 @@
     outs = pl.pallas_call(
         scatter_kernel,
         out_shape=tuple(pltpu.VMEM(query.shape, BF16) for _ in range(4)),
-        in_specs=[any_spec] * 3,
+        in_specs=[any_spec, any_spec, vmem],
         out_specs=[any_spec] * 4,
         scratch_shapes=[
-            tiles(PLANE), tiles(PLANE), tiles(PLANE), tiles(PLANE), tiles(AHEAD), tiles(PLANE),
-            tiles(PLANE), tiles(PLANE), pltpu.VMEM((2, BLK, DH), F32),
-            dma, dma, dma((2,)), dma((4,)), dma,
+            tiles(PLANE), tiles(PLANE), tiles(PLANE), tiles(AHEAD), tiles(PLANE), tiles(PLANE),
+            pltpu.VMEM((2, BLK, DH), F32),
+            dma((2,)), dma((4,)), dma,
             dma, dma((PLANE,)), dma, dma((PLANE,)), dma, dma((PLANE,)), dma, dma((AHEAD,)),
         ],
         compiler_params=pltpu.CompilerParams(

time: 67.6 us -> 68.5 us (1.013)
  Pallas kernels: 66.1 us -> 67.1 us
    pallas_call x1, Pallas kernels: 54.2 us -> 55.2 us  [per_device(): pl.pallas_call(scatter_kernel, out_shape=tuple((pltpu.VMEM(query.shape, B...]
where the time goes in v4:
time: 68.5 us; the launch traced here: 68.4 us
  Pallas kernels  67.1 us (98%)
  between operations  1.3 us (2%)
    pallas_call x1, Pallas kernels, per_device(): pl.pallas_call(scatter_kernel, out_shape=tuple((pltpu.VMEM(query.shape, B...  55.2 us
    pallas_call x1, Pallas kernels, per_device(): pl.pallas_call(gather_kernel, out_shape=(pltpu.VMEM((rows, DH), BF16), pl...  10.3 us

profile of v4, /device:TPU:102, one launch (start us, length us, event | category | flops | bytes accessed | tf_op | source)
XLA Modules:
  0.0 68.4 jit_solution(5704848995122259779)
XLA Ops:
  1.3 10.3 %gather.1 = (bf16[1024,128]{1,0:T(8,128)(2,1)S(1)}, bf16[1024,128]{1,0:T(8,128)(2,1)S(1)}, bf16[32,2,128,128]{3,2,1,0:T(8,128)(2,1)S(1)}, s32[5]{0:T(128)S(1)}) custom-call(bf16[128,640]{1,0:T(8,128)(2,1)} %q_ref.1, bf16[128,640]{1,0:T(8,128)(2,1)} %k_ref.1, bf16[128,640]{1,0:T(8,128)(2,1)} %v_ref.1, bf16[128,640]{1,0:T(8,128)(2,1)} %do_ref.1, s32[5]{0:T(128)} %w_ref.1), custom_call_target="tpu_custom_call" | custom-call | tf_op jit(solution)/shard_map/gather/pallas_call | solution.py:438
  11.6 0.7 %attend.1 = (bf16[1024,128]{1,0:T(8,128)(2,1)S(1)}, bf16[1024,128]{1,0:T(8,128)(2,1)S(1)}, bf16[32,2,128,128]{3,2,1,0:T(8,128)(2,1)S(1)}) custom-call(s32[32]{0:T(128)} %fid_ref.1, s32[1]{0:T(128)S(6)} %copy.11.sink_ref, s32[5]{0:T(128)S(1)} %get-tuple-element.15.w_ref, bf16[1024,128]{1,0:T(8,128)(2,1)S(1)} %get-tuple-element.16.q_ref, ...), custom_call_target="tpu_custom_call" | custom-call | tf_op jit(solution)/shard_map/attend/pallas_call | solution.py:457
  12.4 55.2 %scatter.1 = (bf16[128,640]{1,0:T(8,128)(2,1)S(1)}, bf16[128,640]{1,0:T(8,128)(2,1)S(1)}, bf16[128,640]{1,0:T(8,128)(2,1)S(1)}, bf16[128,640]{1,0:T(8,128)(2,1)S(1)}) custom-call(bf16[1024,128]{1,0:T(8,128)(2,1)S(1)} %get-tuple-element.19.att_ref, bf16[1024,128]{1,0:T(8,128)(2,1)S(1)} %get-tuple-element.20.dq_ref, ...), custom_call_target="tpu_custom_call" | custom-call | tf_op jit(solution)/shard_map/scatter/pallas_call | solution.py:479
  67.5 0.9 %finish.1 = (bf16[128,640]{1,0:T(8,128)(2,1)}, bf16[128,640]{1,0:T(8,128)(2,1)}, bf16[128,640]{1,0:T(8,128)(2,1)}, bf16[128,640]{1,0:T(8,128)(2,1)}) custom-call(bf16[128,640]{1,0:T(8,128)(2,1)S(1)} %get-tuple-element.22.refs_0_, bf16[128,640]{1,0:T(8,128)(2,1)S(1)} %get-tuple-element.23.refs_1_, bf16[128,640]{1,0:T(8,128)(2,1)S(1)} %get-tuple-element.24.refs_2_, ...), custom_call_target="tpu_custom_call" | custom-call | tf_op jit(solution)/shard_map/finish/pallas_call | solution.py:495

commit v5 on v4

--- a/solution.py
+++ b/solution.py
@@ -17,7 +17,7 @@
 NBLK = RING * PLANE
 BF16 = jnp.bfloat16
 F32 = jnp.float32
-TILE_Q = 2 * BLK
+TILE_Q = 4 * BLK
 MAX_CHUNKS = 5
 NEG = -1e30
 MIB = 1 << 20
@@ -231,12 +231,11 @@
             near = (frame <= query_frame) & (frame > query_frame - win)
             return near | ((frame == sink) & (sink <= query_frame))
 
-        @pl.loop(0, PLANE // 2)
+        @pl.loop(0, PLANE // 4)
         def _(t):
             rows = pl.ds(pl.multiple_of(t * TILE_Q, TILE_Q), TILE_Q)
-            block_a = y * PLANE + 2 * t
-            frame_a = (block_a + c) // 4
-            frame_b = (block_a + 1 + c) // 4
+            frame_a = (y * PLANE + 4 * t + c) // 4
+            frame_b = frame_a + 1
             low = jnp.maximum(frame_a - win + 1, 0)
             near_count = frame_b - low + 1
             count = near_count + (sink < low).astype(jnp.int32)
@@ -260,7 +259,7 @@
                 for k in range(4):
                     here = (start + k + c) // 4 == frame
                     bias = jnp.where(
-                        lane < BLK,
+                        lane < (4 - c) * BLK,
                         jnp.where(here & see_a, 0.0, NEG),
                         jnp.where(here & see_b, 0.0, NEG),
                     )

time: 68.5 us -> 66.7 us (0.974); the launches traced: 68.4 us -> 65.9 us
  Pallas kernels: 67.1 us -> 64.6 us
    pallas_call x1, Pallas kernels: 55.2 us -> 52.7 us  [per_device(): pl.pallas_call(scatter_kernel, out_shape=tuple((pltpu.VMEM(query.shape, B...]
where the time goes in v5:
time: 66.7 us; the launch traced here: 65.9 us
  Pallas kernels  64.6 us (97%)
  between operations  1.3 us (2%)
    pallas_call x1, Pallas kernels, per_device(): pl.pallas_call(scatter_kernel, out_shape=tuple((pltpu.VMEM(query.shape, B...  52.7 us
    pallas_call x1, Pallas kernels, per_device(): pl.pallas_call(gather_kernel, out_shape=(pltpu.VMEM((rows, DH), BF16), pl...  10.3 us

profile of v5, /device:TPU:102, one launch (start us, length us, event | category | flops | bytes accessed | tf_op | source)
XLA Modules:
  0.0 65.9 jit_solution(1520747196275033228)
XLA Ops:
  1.3 10.3 %gather.1 = (bf16[1024,128]{1,0:T(8,128)(2,1)S(1)}, bf16[1024,128]{1,0:T(8,128)(2,1)S(1)}, bf16[32,2,128,128]{3,2,1,0:T(8,128)(2,1)S(1)}, s32[5]{0:T(128)S(1)}) custom-call(bf16[128,640]{1,0:T(8,128)(2,1)} %q_ref.1, bf16[128,640]{1,0:T(8,128)(2,1)} %k_ref.1, bf16[128,640]{1,0:T(8,128)(2,1)} %v_ref.1, bf16[128,640]{1,0:T(8,128)(2,1)} %do_ref.1, s32[5]{0:T(128)} %w_ref.1), custom_call_target="tpu_custom_call" | custom-call | tf_op jit(solution)/shard_map/gather/pallas_call | solution.py:437
  11.6 0.7 %attend.1 = (bf16[1024,128]{1,0:T(8,128)(2,1)S(1)}, bf16[1024,128]{1,0:T(8,128)(2,1)S(1)}, bf16[32,2,128,128]{3,2,1,0:T(8,128)(2,1)S(1)}) custom-call(s32[32]{0:T(128)} %fid_ref.1, s32[1]{0:T(128)S(6)} %copy.11.sink_ref, s32[5]{0:T(128)S(1)} %get-tuple-element.15.w_ref, bf16[1024,128]{1,0:T(8,128)(2,1)S(1)} %get-tuple-element.16.q_ref, ...), custom_call_target="tpu_custom_call" | custom-call | tf_op jit(solution)/shard_map/attend/pallas_call | solution.py:456
  12.4 52.7 %scatter.1 = (bf16[128,640]{1,0:T(8,128)(2,1)S(1)}, bf16[128,640]{1,0:T(8,128)(2,1)S(1)}, bf16[128,640]{1,0:T(8,128)(2,1)S(1)}, bf16[128,640]{1,0:T(8,128)(2,1)S(1)}) custom-call(bf16[1024,128]{1,0:T(8,128)(2,1)S(1)} %get-tuple-element.19.att_ref, bf16[1024,128]{1,0:T(8,128)(2,1)S(1)} %get-tuple-element.20.dq_ref, ...), custom_call_target="tpu_custom_call" | custom-call | tf_op jit(solution)/shard_map/scatter/pallas_call | solution.py:478
  65.0 0.9 %finish.1 = (bf16[128,640]{1,0:T(8,128)(2,1)}, bf16[128,640]{1,0:T(8,128)(2,1)}, bf16[128,640]{1,0:T(8,128)(2,1)}, bf16[128,640]{1,0:T(8,128)(2,1)}) custom-call(bf16[128,640]{1,0:T(8,128)(2,1)S(1)} %get-tuple-element.22.refs_0_, bf16[128,640]{1,0:T(8,128)(2,1)S(1)} %get-tuple-element.23.refs_1_, bf16[128,640]{1,0:T(8,128)(2,1)S(1)} %get-tuple-element.24.refs_2_, ...), custom_call_target="tpu_custom_call" | custom-call | tf_op jit(solution)/shard_map/finish/pallas_call | solution.py:494
